TPU v7x, 32 devices: a whole 2x2x4 slice. The times are simulated.
32 devices in a mesh: section: 4 (over x, core), shard: 4 (over z), replica: 2 (over y).
Axes of the slice: x: 2, y: 2, z: 4, core: 2. Of those that a mesh axis runs over, the one named last changes fastest.
Arguments:
- normed: bfloat16 [4, 2, 1024, 4096], P('section', None, ('shard', 'replica')), may hold values from -0.125 to 0.125
- key_cotangent: bfloat16 [4, 2, 1024, 512], P('section', None, ('shard', 'replica')), may hold values from -12 to 12
- positions: int32 [2, 1024], P(None, ('shard', 'replica')), may hold values from 0 to 1023, as said below
- key_weight: bfloat16 [4, 4096, 512], P('section', 'shard'), may hold values from -0.09375 to 0.09375
Outputs:
- key_weight_grad: bfloat16 [4, 4096, 512], P('section', 'shard')
- passed_grad: bfloat16 [4, 2, 1024, 4096], P('section', None, ('shard', 'replica'))
Inputs may be any that keep to these rules, and one draw needn't show every extreme that they name: `positions`: each token's position within its document of the micro-batch; in every micro-batch a document begins at every multiple of 1024 tokens, and in all but the first micro-batch at further places drawn at random.
All inputs are finite; a program needn't handle non-finite values.
Results may differ from a plain program's by a relative error of at most 0.018.
Values may be sent and summed in bfloat16 or wider, within the bound.
No kernel may reach another device: no remote copies, remote signals or barrier semaphores. Data moves between devices by JAX's collectives and lax.ppermute only.
A program may use at most 64 MiB of HBM per device.

v0:
```python
import jax
import jax.numpy as jnp
from jax import lax
from jax.sharding import PartitionSpec as P

HEAD = 128


def shifted(value, axis, steps):
    count = lax.axis_size(axis)
    leading, last = (max(0, -steps), min(count, count - steps))
    return lax.ppermute(value, axis, [(source, source + steps) for source in range(leading, last)])


def undo_rotation(cotangent, positions):
    half = HEAD // 2
    heads = cotangent.shape[-1] // HEAD
    index = jnp.arange(half, dtype=jnp.float32)
    freq = jnp.power(jnp.float32(500000.0), -2.0 * index / HEAD)
    angle = positions.astype(jnp.float32)[..., None] * freq
    angle = jnp.concatenate([angle, angle], axis=-1)[:, :, None, :]
    cosine = jnp.cos(angle)
    sine = jnp.sin(angle)
    lead = cotangent.shape[:2]
    grads = cotangent.astype(jnp.float32).reshape(lead + (heads, HEAD))
    swapped = jnp.concatenate([grads[..., half:], -grads[..., :half]], axis=-1)
    result = grads * cosine + swapped * sine
    return result.reshape(lead + (heads * HEAD,)).astype(jnp.bfloat16)


def per_device(normed, key_cotangent, positions, key_weight):
    key_grad = undo_rotation(key_cotangent[0], positions)
    width = normed.shape[3]
    local_rows = key_weight[0]
    partial_cols = jnp.einsum(
        "mtk,dk->mtd",
        lax.all_gather(key_grad, "shard", axis=1, tiled=True),
        local_rows,
        preferred_element_type=jnp.float32,
    ).astype(jnp.bfloat16)
    moved = lax.all_to_all(partial_cols, "shard", split_axis=1, concat_axis=2, tiled=True)
    input_grad = moved[:, :, :width][None]
    passed = shifted(input_grad, "section", -1)
    steps_tok = normed.shape[1] * normed.shape[2]
    flat_in = normed[0].reshape(steps_tok, width)
    flat_key = key_grad.reshape(steps_tok, key_grad.shape[-1])
    padding = lax.axis_size("shard") * local_rows.shape[0] - width
    padded = jnp.pad(flat_in, ((0, 0), (0, padding)))
    shard_total = lax.psum_scatter(
        lax.dot_general(
            padded, flat_key, (((0,), (0,)), ((), ())), preferred_element_type=jnp.float32
        ).astype(jnp.bfloat16),
        "shard",
        scatter_dimension=0,
        tiled=True,
    )
    shard_round = lax.optimization_barrier(shard_total).astype(jnp.float32)
    total = lax.psum(shard_round.astype(jnp.bfloat16), "replica")
    return (total[None], passed)


def solution(mesh):
    in_specs = (
        P("section", None, ("shard", "replica"), None),
        P("section", None, ("shard", "replica"), None),
        P(None, ("shard", "replica")),
        P("section", "shard", None),
    )
    out_specs = (P("section", "shard", None), P("section", None, ("shard", "replica"), None))
    return jax.shard_map(
        per_device, mesh=mesh, in_specs=in_specs, out_specs=out_specs, check_vma=False
    )
```

profile of v0, /device:TPU:0, one launch (start us, length us, event | category | flops | bytes accessed | tf_op | source)
XLA Modules:
  0.0 222.6 jit_solution(9915633863694696768)
XLA Ops:
  7.2 1.3 reshape.72
  8.5 0.7 convert_element_type.52
  9.2 0.1 broadcast_multiply_fusion
  9.3 0.5 fusion.6
  9.8 0.4 fusion.8
  10.2 0.5 add_convert_fusion
  10.7 0.2 mul.71
  10.9 0.9 mul.65
  11.8 1.3 mul.69
  13.0 1.8 fusion.3
  14.9 0.0 reduce-scatter.2.cloned.1.call-start
  14.9 3.2 %fusion = bf16[4096,512]{0,1:T(8,128)(2,1)} fusion(bf16[256,4096]{1,0:T(8,128)(2,1)S(1)} %bitcast.26, bf16[32,8,4,128]{3,2,1,0:T(4,128)(2,1)S(1)} %bitcast.28), kind=kOutput, calls=%fused_computation.1 | convolution fusion | flops 1075838976 | bytes 6553600 | tf_op jit(solution)/shard_map/dot_general | solution.py:50
  18.2 0.0 all-reduce.2.cloned.1.call-start
  18.2 27.5 %all-gather.2.cloned.1.call-done = bf16[2,512,512]{2,1,0:T(8,128)(2,1)} async-done(((bf16[2,128,512]{2,1,0:T(8,128)(2,1)}), bf16[2,512,512]{2,1,0:T(8,128)(2,1)}) %all-gather.2.cloned.1.call-update) | async-done | bytes 1048592 | tf_op jit(solution)/shard_map/all_gather | solution.py:37
  45.7 2.5 %convolution_convert_fusion.1 = bf16[2,512,1024]{2,1,0:T(8,128)(2,1)S(1)} fusion(bf16[2,512,512]{2,1,0:T(8,128)(2,1)} %all-gather.2.cloned.1.call-done, bf16[1,1024,512]{2,1,0:T(8,128)(2,1)S(1)} %copy-done.1), kind=kOutput, calls=%fused_computation.2 | convolution fusion | flops 1074790400 | bytes 4194304 | tf_op jit(solution)/shard_map/mtk,dk->mtd/dot_general | solution.py:35
  48.2 2.2 copy.8
  50.4 107.6 %all_to_all.15 = bf16[2,512,1024]{2,0,1:T(2,128)(2,1)S(1)} all-to-all(bf16[2,512,1024]{2,0,1:T(2,128)(2,1)S(1)} %copy.8), channel_id=1, replica_groups=mesh['section'=4,'shard'=4,'replica'=2] {'shard'}, dimensions={1} | all-to-all | bytes 4194304 | tf_op jit(solution)/shard_map/all_to_all | solution.py:41
  158.0 2.9 %copy.9 = bf16[2,128,4,1024]{3,2,1,0:T(4,128)(2,1)} copy(bf16[2,128,4,1024]{3,0,1,2:T(2,128)(2,1)S(1)} %bitcast.27) | data formatting | bytes 4194304 | tf_op jit(solution)/shard_map/all_to_all | solution.py:41
  161.0 4.5 %broadcast_in_dim.10 = bf16[1,2,128,4096]{3,2,1,0:T(8,128)(2,1)} reshape(bf16[2,128,4,1024]{3,2,1,0:T(4,128)(2,1)} %copy.9) | data formatting | bytes 4194304 | tf_op jit(solution)/shard_map/broadcast_in_dim | solution.py:42
  165.5 1.3 collective-permute-start
  166.9 5.0 %collective-permute-done = bf16[1,2,128,4096]{3,2,1,0:T(8,128)(2,1)} collective-permute-done((bf16[1,2,128,4096]{3,2,1,0:T(8,128)(2,1)}, bf16[1,2,128,4096]{3,2,1,0:T(8,128)(2,1)}, u32[]{:S(2)}, u32[]{:S(2)}) %collective-permute-start) | collective-permute-done | bytes 2097184 | tf_op jit(solution)/shard_map/ppermute | solution.py:12
  171.9 38.7 %all-reduce.2.cloned.1.call-done = bf16[1,1024,512]{1,2,0:T(8,128)(2,1)} async-done(((bf16[1,1024,512]{1,2,0:T(8,128)(2,1)}), bf16[1,1024,512]{1,2,0:T(8,128)(2,1)}) %all-reduce.2.cloned.1.call-update) | async-done | bytes 1048592 | tf_op jit(solution)/shard_map/psum | solution.py:58
  210.6 2.3 %copy.10 = bf16[1,1024,512]{2,1,0:T(8,128)(2,1)} copy(bf16[1,1024,512]{1,2,0:T(8,128)(2,1)} %all-reduce.2.cloned.1.call-done) | data formatting | bytes 2097152
  212.9 3.1 %copy.18 = bf16[1,2,128,4096]{3,2,1,0:T(8,128)(2,1)} copy(bf16[1,2,128,4096]{3,2,1,0:T(8,128)(2,1)} %collective-permute-done) | data formatting | bytes 4194304
  (10 shorter events, 0.1 us)
Async XLA Ops:
  7.2 7.7 %copy-start = (bf16[1,2,128,4096]{3,2,1,0:T(8,128)(2,1)S(1)}, bf16[1,2,128,4096]{3,2,1,0:T(8,128)(2,1)}, u32[]{:S(2)}) copy-start(bf16[1,2,128,4096]{3,2,1,0:T(8,128)(2,1)} %param.4) | copy-start | bytes 6291460
  7.2 38.5 %all-gather.2.cloned.1.call-start = ((), (), s32[]{:S(2)}) async-start(), calls=%async_computation.4 | async-start | bytes 1310720 | tf_op jit(solution)/shard_map/all_gather | solution.py:37
  14.9 152.0 %reduce-scatter.2.cloned.1.call-start = ((), (), s32[]{:S(2)}) async-start(), calls=%async_computation.2 | async-start | bytes 5242880 | tf_op jit(solution)/shard_map/reduce_scatter | solution.py:49
  18.2 27.6 %copy-start.1 = (bf16[1,1024,512]{2,1,0:T(8,128)(2,1)S(1)}, bf16[1,1024,512]{2,1,0:T(8,128)(2,1)}, u32[]{:S(2)}) copy-start(bf16[1,1024,512]{2,1,0:T(8,128)(2,1)} %param.7) | copy-start | bytes 3145732
  18.2 192.5 %all-reduce.2.cloned.1.call-start = ((), (), s32[]{:S(2)}) async-start(), calls=%async_computation.3 | async-start | bytes 2097152 | tf_op jit(solution)/shard_map/psum | solution.py:58
  165.5 6.4 %collective-permute-start = (bf16[1,2,128,4096]{3,2,1,0:T(8,128)(2,1)}, bf16[1,2,128,4096]{3,2,1,0:T(8,128)(2,1)}, u32[]{:S(2)}, u32[]{:S(2)}) collective-permute-start(bf16[1,2,128,4096]{3,2,1,0:T(8,128)(2,1)} %broadcast_in_dim.10), channel_id=1, source_target_pairs={{8,0},{16,8},{24,16},{9,1},{17,9},{25,17},{10,2},{18,10},{26,18},{... | collective-permute-start | bytes 6291464 | tf_op jit(solution)/shard_map/ppermute | solution.py:12
Sparse Core Ops, SparseCore 0:
  15.0 30.6 all-gather.1
  48.0 115.0 reduce-scatter.1
  167.0 43.6 all-reduce.1
where the time goes:
time: 223 us
  blocking collectives  108 us (48%)
  waiting for transfers between devices  71.4 us (32%)
  local copies, waits for them, and re-layouts  18.6 us (8%)
  between operations  13.8 us (6%)
  matrix products  5.74 us (3%)
  other arithmetic  3.96 us (2%)
    all_to_all x1, blocking collectives, per_device(): lax.all_to_all(partial_cols, 'shard', split_axis=1, concat_axis=2, tiled=...  108 us
    psum x1, waiting for transfers between devices, per_device(): total = lax.psum(shard_round.astype(jnp.bfloat16), 'replica')  38.7 us
    all_gather x1, waiting for transfers between devices, per_device(): lax.all_gather(key_grad, 'shard', axis=1, tiled=True)  27.5 us
    unnamed x6, local copies, waits for them, and re-layouts  5.41 us
    ppermute x1, waiting for transfers between devices, shifted(): lax.ppermute(value, axis, [(source, source + steps) for source in range(l...  5.04 us
    broadcast_in_dim x1, local copies, waits for them, and re-layouts, per_device(): input_grad = moved[:, :, :width][None]  4.53 us
  transfers between devices with their start and end apart: 4, of which 3 were waited for; matrix products, arithmetic and copies ran while one was open for 7% of the time, Pallas kernels for 0%

commit v1 on v0

v1 whole, which is shorter than its diff:
```python
import functools

import jax
import numpy as np
import jax.numpy as jnp
from jax import lax
from jax.experimental import pallas as pl
from jax.experimental.pallas import tpu as pltpu
from jax.sharding import PartitionSpec as P


HEAD = 128
AXES = ("section", "shard", "replica")
BF16 = jnp.bfloat16
F32 = jnp.float32


def shifted(value, axis, steps):
    count = lax.axis_size(axis)
    leading, last = (max(0, -steps), min(count, count - steps))
    return lax.ppermute(value, axis, [(source, source + steps) for source in range(leading, last)])


def undo_rotation(cotangent, positions):
    half = HEAD // 2
    heads = cotangent.shape[-1] // HEAD
    index = jnp.arange(half, dtype=F32)
    freq = jnp.power(F32(500000.0), -2.0 * index / HEAD)
    angle = positions.astype(F32)[..., None] * freq
    angle = jnp.concatenate([angle, angle], axis=-1)[:, :, None, :]
    cosine = jnp.cos(angle)
    sine = jnp.sin(angle)
    lead = cotangent.shape[:2]
    grads = cotangent.astype(F32).reshape(lead + (heads, HEAD))
    swapped = jnp.concatenate([grads[..., half:], -grads[..., :half]], axis=-1)
    result = grads * cosine + swapped * sine
    return result.reshape(lead + (heads * HEAD,)).astype(BF16)


def general_device(normed, key_cotangent, positions, key_weight):
    key_grad = undo_rotation(key_cotangent[0], positions)
    width = normed.shape[3]
    local_rows = key_weight[0]
    partial_cols = jnp.einsum(
        "mtk,dk->mtd",
        lax.all_gather(key_grad, "shard", axis=1, tiled=True),
        local_rows,
        preferred_element_type=F32,
    ).astype(BF16)
    moved = lax.all_to_all(partial_cols, "shard", split_axis=1, concat_axis=2, tiled=True)
    input_grad = moved[:, :, :width][None]
    passed = shifted(input_grad, "section", -1)
    steps_tok = normed.shape[1] * normed.shape[2]
    flat_in = normed[0].reshape(steps_tok, width)
    flat_key = key_grad.reshape(steps_tok, key_grad.shape[-1])
    padding = lax.axis_size("shard") * local_rows.shape[0] - width
    padded = jnp.pad(flat_in, ((0, 0), (0, padding)))
    shard_total = lax.psum_scatter(
        lax.dot_general(
            padded, flat_key, (((0,), (0,)), ((), ())), preferred_element_type=F32
        ).astype(BF16),
        "shard",
        scatter_dimension=0,
        tiled=True,
    )
    total = lax.psum(shard_total, "replica")
    return (total[None], passed)


VMEM_GRANT = 12 * 2**20


def call(body, out_shape, ids, *args, blocks=None, place=None, aliases=None, scratch=(), grant=VMEM_GRANT, flops=0):
    spec = pl.BlockSpec(memory_space=pltpu.VMEM)
    blocks = blocks or {}
    nbytes = sum(a.size * a.dtype.itemsize for i, a in enumerate(args) if i not in blocks)
    in_specs = [blocks.get(i, spec) for i in range(len(args))]
    whole = place or pl.BlockSpec(out_shape.shape, lambda i, ids: (0,) * len(out_shape.shape))
    in_specs = [
        pl.BlockSpec(a.shape, lambda i, ids, n=len(a.shape): (0,) * n) if s is spec else s
        for a, s in zip(args, in_specs)
    ]
    return pl.pallas_call(
        body,
        out_shape=out_shape,
        grid_spec=pltpu.PrefetchScalarGridSpec(
            num_scalar_prefetch=1, grid=(1,), in_specs=in_specs, out_specs=whole,
            scratch_shapes=scratch,
        ),
        compiler_params=pltpu.CompilerParams(vmem_limit_bytes=grant),
        input_output_aliases=aliases or {},
        cost_estimate=pl.CostEstimate(flops=flops, bytes_accessed=nbytes, transcendentals=0),
    )(ids, *args)


def block_of(flat, half, slot):
    return pl.BlockSpec((flat.shape[0], half), lambda i, ids: (0, ids[slot]))


def rotate_body(ids, freq, pos, cot, out):
    micro, tokens = pos.shape
    lane = lax.broadcasted_iota(jnp.int32, (tokens, HEAD), 1)
    for m in range(micro):
        rows = pl.ds(m * tokens, tokens)
        place = jnp.broadcast_to(pos[pl.ds(m, 1), :].astype(F32), (HEAD, tokens))
        angle = jnp.transpose(place) * freq[...]
        cosine = jnp.cos(angle)
        sine = jnp.sin(angle)
        sine = jnp.where(lane < HEAD // 2, sine, -sine)
        for h in range(cot.shape[1] // HEAD):
            cols = pl.ds(h * HEAD, HEAD)
            grad = cot[rows, cols].astype(F32)
            out[rows, cols] = (
                grad * cosine + pltpu.roll(grad, HEAD // 2, 1) * sine
            ).astype(out.dtype)


def copy_body(ids, *refs):
    *parts, out = refs
    at = 0
    for part in parts:
        out[pl.ds(at, part.shape[0]), :] = part[...]
        at += part.shape[0]


def outer(rows, keys):
    return lax.dot_general(rows, keys, (((0,), (0,)), ((), ())), preferred_element_type=F32)


def inner(keys, rows):
    return lax.dot_general(keys, rows, (((1,), (1,)), ((), ())), preferred_element_type=F32)


def term_body(slot, place, ids, normed, ours, theirs, other, *rest):
    *sums, out, rows, sem = rest
    count, half = rows.shape
    cols = pl.ds(pl.multiple_of(ids[slot] * half, half), half)
    fetch = pltpu.make_async_copy(normed.at[:, cols], rows, sem)
    fetch.start()
    total = outer(other[pl.ds(place * count, count), :], theirs[...])
    fetch.wait()
    total = total + outer(rows[...], ours[...])
    for part in sums:
        total = total + part[...].astype(F32)
    out[...] = total.astype(out.dtype)


def share_body(ids, keys, *rest):
    *blocks, out = rest
    count, half = out.shape[0], blocks[0].shape[0]
    for i, block in enumerate(blocks):
        part = inner(keys[pl.ds(count, count), :], block[...])
        out[:, pl.ds(i * half, half)] = part.astype(out.dtype)


def share_pair_body(ids, keys, w2, w4, w3, w5, out):
    count, half = out.shape[0], w2.shape[0]
    for i, (near, far) in enumerate(((w2, w4), (w3, w5))):
        part = inner(keys[pl.ds(count, count), :], near[...] + far[...])
        out[:, pl.ds(i * half, half)] = part.astype(out.dtype)


def passed_body(ids, keys, w0, w1, w2, w4, w3, w5, near, far, out):
    count, half = out.shape[0], w0.shape[0]
    for i in range(4):
        block = (w0, w1)[i][...] if i < 2 else (w2, w3)[i - 2][...] + (w4, w5)[i - 2][...]
        mine = pl.multiple_of(ids[i] * half, half)
        theirs = pl.multiple_of(ids[4 + i] * half, half)
        out[:, pl.ds(mine, half)] = inner(keys[pl.ds(0, count), :], block).astype(out.dtype)
        out[:, pl.ds(theirs, half)] = (near, far)[i // 2][:, pl.ds(i % 2 * half, half)]


def add_body(ids, a, b, out):
    out[...] = (a[...].astype(F32) + b[...].astype(F32)).astype(out.dtype)


def rows_body(ids, mine, theirs, out):
    half = mine.shape[0]
    out[pl.ds(pl.multiple_of(ids[8] * half, half), half), :] = mine[...]
    out[pl.ds(pl.multiple_of((1 - ids[8]) * half, half), half), :] = theirs[...]


def pair_device(normed, key_cotangent, positions, key_weight):
    sections, shards, replicas = (lax.axis_size(a) for a in AXES)
    _, z, y = (lax.axis_index(a) for a in AXES)
    micro, tokens, width = normed.shape[1:]
    count = micro * tokens
    depth = key_cotangent.shape[-1]
    half = key_weight.shape[1] // replicas
    out = lambda *shape: jax.ShapeDtypeStruct(shape, BF16)

    def send(value, line, back=0, swap=0):
        pairs = []
        for a in range(back, sections):
            for b in range(shards):
                for c in range(replicas):
                    if line(b) is not None:
                        target = ((a - back) * shards + line(b)) * replicas + (c ^ swap)
                        pairs.append(((a * shards + b) * replicas + c, target))
        return lax.ppermute(value, AXES, pairs)

    stay = lambda b: b
    flip = lambda b: b ^ 1
    inward = lambda b: {0: 1, 3: 2}.get(b)
    across = lambda b: {1: 2, 2: 1}.get(b)
    outward = lambda b: {1: 0, 2: 3}.get(b)

    last = jnp.where((z == 0) | (z == shards - 1), 3, 2)
    far = jnp.stack([z, z ^ 1, z ^ (5 - last), z ^ last]).astype(jnp.int32) * replicas
    ids = jnp.concatenate([far + y, far + (1 - y), jnp.stack([y, y]).astype(jnp.int32)])

    flat = normed.reshape(count, width)
    index = np.arange(HEAD // 2, dtype=np.float32)
    freq = np.power(np.float32(500000.0), -2.0 * index / HEAD).astype(np.float32)
    freq = jnp.asarray(np.concatenate([freq, freq])[None])

    pack0 = lax.dynamic_slice(flat, (0, ids[7] * half), (count, half))
    other0 = send(pack0, stay, swap=1)
    ours = call(rotate_body, out(count, depth), ids, freq, positions,
                key_cotangent.reshape(count, depth))
    theirs = send(ours, stay, swap=1)
    piece = lax.dynamic_slice(key_weight[0], (y * half, 0), (half, depth))
    w1 = send(piece, flip, back=1)
    w2 = send(piece, across, back=1)
    w0 = send(piece, stay, back=1)
    pack1 = lax.dynamic_slice(flat, (0, ids[6] * half), (count, half))
    other1 = send(pack1, stay, swap=1)
    pack2 = call(copy_body, out(2 * count, half), ids, flat, flat,
                 blocks={0: block_of(flat, half, 5), 1: block_of(flat, half, 4)})
    other2 = send(pack2, stay, swap=1)

    def term(slot, place, other, *sums):
        return call(functools.partial(term_body, slot, place), out(half, depth), ids,
                    flat, ours, theirs, other, *sums, blocks={0: pl.BlockSpec(memory_space=pltpu.HBM)},
                    scratch=[pltpu.VMEM((count, half), BF16), pltpu.SemaphoreType.DMA],
                    flops=4 * count * half * depth)

    def plus(a, b):
        return call(add_body, out(half, depth), ids, a, b)

    term3 = term(3, 0, other0)
    a1 = send(term3, inward)
    w3 = send(w1, across)
    w4 = send(w2, outward)
    both = call(copy_body, out(2 * count, depth), ids, ours, theirs)
    keys = send(both, stay, back=1)
    term2 = term(2, 0, other1)
    a2 = send(term2, inward)
    b1 = send(plus(term3, a1), across)
    w5 = send(w3, outward)
    b2 = send(plus(term2, a2), across)
    c1 = send(term(1, 0, other2, b1), flip)
    near = call(share_body, out(count, 2 * half), ids, keys, w0, w1,
                flops=4 * count * half * depth)
    near = send(near, stay, swap=1)
    far = call(share_pair_body, out(count, 2 * half), ids, keys, w2, w4, w3, w5,
               flops=4 * count * half * depth)
    far = send(far, stay, swap=1)
    mine = term(0, 1, other2, b2, c1)
    rest = send(mine, stay, swap=1)
    passed = call(passed_body, out(count, width), ids, keys, w0, w1, w2, w4, w3, w5, near, far,
                  flops=8 * count * half * depth)
    weight_grad = call(rows_body, out(replicas * half, depth), ids, mine, rest)
    return weight_grad[None], passed.reshape(normed.shape)


def solution(mesh):
    in_specs = (
        P("section", None, ("shard", "replica"), None),
        P("section", None, ("shard", "replica"), None),
        P(None, ("shard", "replica")),
        P("section", "shard", None),
    )
    out_specs = (P("section", "shard", None), P("section", None, ("shard", "replica"), None))

    def body(normed, key_cotangent, positions, key_weight):
        pairs = (
            mesh.shape["shard"] == 4
            and mesh.shape["replica"] == 2
            and key_weight.shape[1] * 4 == normed.shape[3]
            and key_weight.shape[1] % 1024 == 0
        )
        form = pair_device if pairs else general_device
        return form(normed, key_cotangent, positions, key_weight)

    return jax.shard_map(body, mesh=mesh, in_specs=in_specs, out_specs=out_specs, check_vma=False)
```

time: 223 us -> 110 us (0.49)
  blocking collectives: 108 us -> 0 us
  starting transfers between devices: 1.4 us -> 39.9 us
  waiting for transfers between devices: 71.4 us -> 43.4 us
  Pallas kernels: 0 us -> 19 us
  local copies, waits for them, and re-layouts: 18.6 us -> 4.94 us
  between operations: 13.8 us -> 2.22 us
  matrix products: 5.74 us -> 0 us
  other arithmetic: 3.96 us -> 0.16 us
    all_to_all x1 -> x0, blocking collectives: 108 us -> none  [per_device(): lax.all_to_all(partial_cols, 'shard', split_axis=1, concat_axis=2, tiled=...]
    psum x1 -> x0, waiting for transfers between devices: 38.7 us -> none  [per_device(): total = lax.psum(shard_round.astype(jnp.bfloat16), 'replica')]
    ppermute x1 -> x19, starting transfers between devices: 1.28 us -> 39.9 us  [send(): return lax.ppermute(value, AXES, pairs)]
    ppermute x1 -> x19, waiting for transfers between devices: 5.04 us -> 43.4 us  [send(): return lax.ppermute(value, AXES, pairs)]
    all_gather x1 -> x0, waiting for transfers between devices: 27.5 us -> none  [per_device(): lax.all_gather(key_grad, 'shard', axis=1, tiled=True)]
    pallas_call x0 -> x13, Pallas kernels: none -> 19 us  [call(): pl.pallas_call(body, out_shape=out_shape, grid_spec=pltpu.PrefetchScalarG...]
    dot_general x2 -> x0, matrix products: 5.74 us -> none  [the longest x1 3.23 us: per_device(): lax.dot_general(padded, flat_key, (((0,), (0,)), ((), ())), preferred_ele...]
    broadcast_in_dim x1 -> x0, local copies, waits for them, and re-layouts: 4.53 us -> none  [per_device(): input_grad = moved[:, :, :width][None]]
  transfers between devices with their start and end apart: 4 -> 19, of which waited for: 3 -> 9; matrix products, arithmetic and copies ran while one was open for 7% -> 2% of each run, Pallas kernels for 0% -> 15%
where the time goes in v1:
time: 110 us
  waiting for transfers between devices  43.4 us (39%)
  starting transfers between devices  39.9 us (36%)
  Pallas kernels  19 us (17%)
  local copies, waits for them, and re-layouts  4.94 us (4%)
  between operations  2.22 us (2%)
    ppermute x19, waiting for transfers between devices, send(): return lax.ppermute(value, AXES, pairs)  43.4 us
    ppermute x19, starting transfers between devices, send(): return lax.ppermute(value, AXES, pairs)  39.9 us
    pallas_call x13, Pallas kernels, call(): pl.pallas_call(body, out_shape=out_shape, grid_spec=pltpu.PrefetchScalarG...  19 us
    unnamed x12, local copies, waits for them, and re-layouts  2.46 us
  transfers between devices with their start and end apart: 19, of which 9 were waited for; matrix products, arithmetic and copies ran while one was open for 2% of the time, Pallas kernels for 15%

profile of v1, /device:TPU:0, one launch (start us, length us, event | category | flops | bytes accessed | tf_op | source)
XLA Modules:
  0.0 109.6 jit_solution(1479138445739746383)
XLA Ops:
  4.5 3.1 %collective-permute-start = (bf16[256,512]{1,0:T(8,128)(2,1)S(1)}, bf16[256,512]{1,0:T(8,128)(2,1)}, u32[]{:S(2)}, u32[]{:S(2)}) collective-permute-start(bf16[256,512]{1,0:T(8,128)(2,1)S(1)} %shard_map.68.ours.refs_0_), channel_id=1, source_target_pairs={{0,1},{1,0},{2,3},{3,2},{4,5},{5,4},{6,7},{7,6},{8,9},{9,8},{10,11... | collective-permute-start | bytes 786440 | tf_op jit(solution)/shard_map/ppermute | solution.py:200
  9.4 1.9 %constant_dynamic-slice_fusion = (bf16[256,512]{1,0:T(8,128)(2,1)}, bf16[256,512]{1,0:T(8,128)(2,1)}) fusion(bf16[256,4096]{1,0:T(8,128)(2,1)} %bitcast.13, s32[]{:T(128)S(6)} %select_n.15, s32[]{:T(128)S(6)} %select_n.14), kind=kLoop, calls=%fused_computation.1 | loop fusion | bytes 1048584 | tf_op jit(solution)/shard_map/dynamic_slice | solution.py:217
  11.4 1.4 %collective-permute-start.12 = (bf16[512,512]{1,0:T(8,128)(2,1)S(1)}, bf16[512,512]{1,0:T(8,128)(2,1)S(1)}, u32[]{:S(2)}, u32[]{:S(2)}) collective-permute-start(bf16[512,512]{1,0:T(8,128)(2,1)S(1)} %dynamic-slice_bitcast_fusion), channel_id=1, source_target_pairs={{8,2},{9,3},{10,0},{11,1},{12,6},{13,7},{14,4},{15,5},{16,10},{17,... | collective-permute-start | bytes 1572872 | tf_op jit(solution)/shard_map/ppermute | solution.py:200
  12.8 1.4 %collective-permute-done.theirs.refs_1_ = bf16[256,512]{1,0:T(8,128)(2,1)} collective-permute-done((bf16[256,512]{1,0:T(8,128)(2,1)S(1)}, bf16[256,512]{1,0:T(8,128)(2,1)}, u32[]{:S(2)}, u32[]{:S(2)}) %collective-permute-start) | collective-permute-done | bytes 262176 | tf_op jit(solution)/shard_map/ppermute | solution.py:200
  14.2 5.3 %collective-permute-done.5.other = bf16[256,512]{1,0:T(8,128)(2,1)} collective-permute-done((bf16[256,512]{1,0:T(8,128)(2,1)}, bf16[256,512]{1,0:T(8,128)(2,1)}, u32[]{:S(2)}, u32[]{:S(2)}) %collective-permute-start.5) | collective-permute-done | bytes 262176 | tf_op jit(solution)/shard_map/ppermute | solution.py:200
  19.6 2.1 %shard_map.72.a = bf16[512,512]{1,0:T(8,128)(2,1)S(1)} custom-call(s32[10]{0:T(128)S(1)} %pad_add_fusion.ids, bf16[256,4096]{1,0:T(8,128)(2,1)S(1)} %bitcast.14, bf16[256,512]{1,0:T(8,128)(2,1)S(1)} %shard_map.68.ours.refs_0_, bf16[256,512]{1,0:T(8,128)(2,1)} %collective-permute-done.theirs.refs_1_, bf16[256,512]{1,0:T(8,128)(2,1)} %collective-permute-done.5.other), custom_call_target="tpu_custom_call" | custom-call | flops 268435456 | bytes 786432 | tf_op jit(solution)/shard_map/pallas_call | solution.py:83
  21.7 3.7 %collective-permute-start.6 = (bf16[512,512]{1,0:T(8,128)(2,1)S(1)}, bf16[512,512]{1,0:T(8,128)(2,1)S(1)}, u32[]{:S(2)}, u32[]{:S(2)}) collective-permute-start(bf16[512,512]{1,0:T(8,128)(2,1)S(1)} %shard_map.72.a), channel_id=1, source_target_pairs={{0,2},{1,3},{6,4},{7,5},{8,10},{9,11},{14,12},{15,13},{16,18},{17,... | collective-permute-start | bytes 1572872 | tf_op jit(solution)/shard_map/ppermute | solution.py:200
  26.1 1.6 %collective-permute-start.2 = (bf16[256,512]{1,0:T(8,128)(2,1)S(1)}, bf16[256,512]{1,0:T(8,128)(2,1)S(1)}, u32[]{:S(2)}, u32[]{:S(2)}) collective-permute-start(bf16[256,512]{1,0:T(8,128)(2,1)S(1)} %copy-done.5), channel_id=1, source_target_pairs={{0,1},{1,0},{2,3},{3,2},{4,5},{5,4},{6,7},{7,6},{8,9},{9,8},{10,11... | collective-permute-start | bytes 786440 | tf_op jit(solution)/shard_map/ppermute | solution.py:200
  28.9 6.5 %collective-permute-done.2.other = bf16[256,512]{1,0:T(8,128)(2,1)S(1)} collective-permute-done((bf16[256,512]{1,0:T(8,128)(2,1)S(1)}, bf16[256,512]{1,0:T(8,128)(2,1)S(1)}, u32[]{:S(2)}, u32[]{:S(2)}) %collective-permute-start.2) | collective-permute-done | bytes 262176 | tf_op jit(solution)/shard_map/ppermute | solution.py:200
  35.4 2.0 %shard_map.70.a = bf16[512,512]{1,0:T(8,128)(2,1)S(1)} custom-call(s32[10]{0:T(128)S(1)} %pad_add_fusion.ids, bf16[256,4096]{1,0:T(8,128)(2,1)S(1)} %bitcast.17, bf16[256,512]{1,0:T(8,128)(2,1)S(1)} %shard_map.68.ours.refs_0_, bf16[256,512]{1,0:T(8,128)(2,1)} %collective-permute-done.theirs.refs_1_, bf16[256,512]{1,0:T(8,128)(2,1)S(1)} %collective-permute-done.2.other), custom_call_target="tpu_custom_call" | custom-call | flops 268435456 | bytes 786432 | tf_op jit(solution)/shard_map/pallas_call | solution.py:83
  42.1 1.5 %shard_map.77 = bf16[512,512]{1,0:T(8,128)(2,1)S(1)} custom-call(s32[10]{0:T(128)S(1)} %pad_add_fusion.ids, bf16[256,512]{1,0:T(8,128)(2,1)S(1)} %shard_map.68.ours.refs_0_, bf16[256,512]{1,0:T(8,128)(2,1)} %collective-permute-done.theirs.refs_1_), custom_call_target="tpu_custom_call" | custom-call | bytes 524288 | tf_op jit(solution)/shard_map/pallas_call | solution.py:83
  45.8 4.2 %collective-permute-done.3.b = bf16[512,512]{1,0:T(8,128)(2,1)S(1)} collective-permute-done((bf16[512,512]{1,0:T(8,128)(2,1)S(1)}, bf16[512,512]{1,0:T(8,128)(2,1)S(1)}, u32[]{:S(2)}, u32[]{:S(2)}) %collective-permute-start.3) | collective-permute-done | bytes 524320 | tf_op jit(solution)/shard_map/ppermute | solution.py:200
  53.9 2.0 %shard_map.74 = bf16[512,512]{1,0:T(8,128)(2,1)S(1)} custom-call(s32[10]{0:T(128)S(1)} %pad_add_fusion.ids, bf16[256,4096]{1,0:T(8,128)(2,1)S(1)} %bitcast.18, bf16[256,512]{1,0:T(8,128)(2,1)S(1)} %shard_map.68.ours.refs_0_, bf16[256,512]{1,0:T(8,128)(2,1)} %collective-permute-done.theirs.refs_1_, bf16[512,512]{1,0:T(8,128)(2,1)S(1)} %collective-permute-done.1.other, ...), custom_call_target="tpu_custom_call" | custom-call | flops 268435456 | bytes 1572864 | tf_op jit(solution)/shard_map/pallas_call | solution.py:83
  56.0 15.6 %collective-permute-start.8 = (bf16[512,512]{1,0:T(8,128)(2,1)S(1)}, bf16[512,512]{1,0:T(8,128)(2,1)S(1)}, u32[]{:S(2)}, u32[]{:S(2)}) collective-permute-start(bf16[512,512]{1,0:T(8,128)(2,1)S(1)} %shard_map.74), channel_id=1, source_target_pairs={{0,2},{1,3},{2,0},{3,1},{4,6},{5,7},{6,4},{7,5},{8,10},{9,11},{10,... | collective-permute-start | bytes 1572872 | tf_op jit(solution)/shard_map/ppermute | solution.py:200
  72.6 1.6 %collective-permute-start.17 = (bf16[256,1024]{1,0:T(8,128)(2,1)S(1)}, bf16[256,1024]{1,0:T(8,128)(2,1)S(1)}, u32[]{:S(2)}, u32[]{:S(2)}) collective-permute-start(bf16[256,1024]{1,0:T(8,128)(2,1)S(1)} %shard_map.78), channel_id=1, source_target_pairs={{0,1},{1,0},{2,3},{3,2},{4,5},{5,4},{6,7},{7,6},{8,9},{9,8},{10,11... | collective-permute-start | bytes 1572872 | tf_op jit(solution)/shard_map/ppermute | solution.py:200
  74.1 3.4 %collective-permute-done.16.w5 = bf16[512,512]{1,0:T(8,128)(2,1)S(1)} collective-permute-done((bf16[512,512]{1,0:T(8,128)(2,1)S(1)}, bf16[512,512]{1,0:T(8,128)(2,1)S(1)}, u32[]{:S(2)}, u32[]{:S(2)}) %collective-permute-start.16) | collective-permute-done | bytes 524320 | tf_op jit(solution)/shard_map/ppermute | solution.py:200
  78.6 1.6 %collective-permute-start.18 = (bf16[256,1024]{1,0:T(8,128)(2,1)S(1)}, bf16[256,1024]{1,0:T(8,128)(2,1)S(1)}, u32[]{:S(2)}, u32[]{:S(2)}) collective-permute-start(bf16[256,1024]{1,0:T(8,128)(2,1)S(1)} %shard_map.79), channel_id=1, source_target_pairs={{0,1},{1,0},{2,3},{3,2},{4,5},{5,4},{6,7},{7,6},{8,9},{9,8},{10,11... | collective-permute-start | bytes 1572872 | tf_op jit(solution)/shard_map/ppermute | solution.py:200
  80.1 8.6 %collective-permute-done.8.rest_1_ = bf16[512,512]{1,0:T(8,128)(2,1)S(1)} collective-permute-done((bf16[512,512]{1,0:T(8,128)(2,1)S(1)}, bf16[512,512]{1,0:T(8,128)(2,1)S(1)}, u32[]{:S(2)}, u32[]{:S(2)}) %collective-permute-start.8) | collective-permute-done | bytes 524320 | tf_op jit(solution)/shard_map/ppermute | solution.py:200
  88.8 2.0 %shard_map.75.mine = bf16[512,512]{1,0:T(8,128)(2,1)S(1)} custom-call(s32[10]{0:T(128)S(1)} %pad_add_fusion.ids, bf16[256,4096]{1,0:T(8,128)(2,1)S(1)} %bitcast.19, bf16[256,512]{1,0:T(8,128)(2,1)S(1)} %shard_map.68.ours.refs_0_, bf16[256,512]{1,0:T(8,128)(2,1)} %collective-permute-done.theirs.refs_1_, bf16[512,512]{1,0:T(8,128)(2,1)S(1)} %collective-permute-done.1.other, ...), custom_call_target="tpu_custom_call" | custom-call | flops 268435456 | bytes 2097152 | tf_op jit(solution)/shard_map/pallas_call | solution.py:83
  90.8 1.6 %collective-permute-start.9 = (bf16[512,512]{1,0:T(8,128)(2,1)S(1)}, bf16[512,512]{1,0:T(8,128)(2,1)S(1)}, u32[]{:S(2)}, u32[]{:S(2)}) collective-permute-start(bf16[512,512]{1,0:T(8,128)(2,1)S(1)} %shard_map.75.mine), channel_id=1, source_target_pairs={{0,1},{1,0},{2,3},{3,2},{4,5},{5,4},{6,7},{7,6},{8,9},{9,8},{10,11... | collective-permute-start | bytes 1572872 | tf_op jit(solution)/shard_map/ppermute | solution.py:200
  92.4 6.2 %collective-permute-done.18.far = bf16[256,1024]{1,0:T(8,128)(2,1)S(1)} collective-permute-done((bf16[256,1024]{1,0:T(8,128)(2,1)S(1)}, bf16[256,1024]{1,0:T(8,128)(2,1)S(1)}, u32[]{:S(2)}, u32[]{:S(2)}) %collective-permute-start.18) | collective-permute-done | bytes 524320 | tf_op jit(solution)/shard_map/ppermute | solution.py:200
  98.7 2.6 %shard_map.80 = bf16[256,4096]{1,0:T(8,128)(2,1)} custom-call(s32[10]{0:T(128)S(1)} %pad_add_fusion.ids, bf16[512,512]{1,0:T(8,128)(2,1)S(1)} %collective-permute-done.10.keys, bf16[512,512]{1,0:T(8,128)(2,1)S(1)} %collective-permute-done.11.rest_0_.w0, bf16[512,512]{1,0:T(8,128)(2,1)S(1)} %collective-permute-done.12.rest_1_.w1, ...), custom_call_target="tpu_custom_call" | custom-call | flops 536870912 | bytes 4718592 | tf_op jit(solution)/shard_map/pallas_call | solution.py:83
  101.3 6.8 %collective-permute-done.9.theirs = bf16[512,512]{1,0:T(8,128)(2,1)S(1)} collective-permute-done((bf16[512,512]{1,0:T(8,128)(2,1)S(1)}, bf16[512,512]{1,0:T(8,128)(2,1)S(1)}, u32[]{:S(2)}, u32[]{:S(2)}) %collective-permute-start.9) | collective-permute-done | bytes 524320 | tf_op jit(solution)/shard_map/ppermute | solution.py:200
  108.0 1.6 %shard_map.76 = bf16[1024,512]{1,0:T(8,128)(2,1)} custom-call(s32[10]{0:T(128)S(1)} %pad_add_fusion.ids, bf16[512,512]{1,0:T(8,128)(2,1)S(1)} %shard_map.75.mine, bf16[512,512]{1,0:T(8,128)(2,1)S(1)} %collective-permute-done.9.theirs), custom_call_target="tpu_custom_call" | custom-call | bytes 1048576 | tf_op jit(solution)/shard_map/pallas_call | solution.py:83
  (45 shorter events, 19.0 us)
Async XLA Ops:
  0.6 10.7 %copy-start = (bf16[1,1024,512]{2,1,0:T(8,128)(2,1)S(1)}, bf16[1,1024,512]{2,1,0:T(8,128)(2,1)}, u32[]{:S(2)}) copy-start(bf16[1,1024,512]{2,1,0:T(8,128)(2,1)} %param.8) | copy-start | bytes 3145732
  0.6 18.9 %copy-start.1 = (bf16[1,2,128,4096]{3,2,1,0:T(8,128)(2,1)S(1)}, bf16[1,2,128,4096]{3,2,1,0:T(8,128)(2,1)}, u32[]{:S(2)}) copy-start(bf16[1,2,128,4096]{3,2,1,0:T(8,128)(2,1)} %param.5) | copy-start | bytes 6291460
  0.8 1.1 %copy-start.2 = (bf16[1,2,128,512]{3,2,1,0:T(8,128)(2,1)S(1)}, bf16[1,2,128,512]{3,2,1,0:T(8,128)(2,1)}, u32[]{:S(2)}) copy-start(bf16[1,2,128,512]{3,2,1,0:T(8,128)(2,1)} %param.6) | copy-start | bytes 786436
  1.9 0.7 copy-start.3
  4.5 9.8 %collective-permute-start = (bf16[256,512]{1,0:T(8,128)(2,1)S(1)}, bf16[256,512]{1,0:T(8,128)(2,1)}, u32[]{:S(2)}, u32[]{:S(2)}) collective-permute-start(bf16[256,512]{1,0:T(8,128)(2,1)S(1)} %shard_map.68.ours.refs_0_), channel_id=1, source_target_pairs={{0,1},{1,0},{2,3},{3,2},{4,5},{5,4},{6,7},{7,6},{8,9},{9,8},{10,11... | collective-permute-start | bytes 786440 | tf_op jit(solution)/shard_map/ppermute | solution.py:200
  11.3 8.3 %collective-permute-start.5 = (bf16[256,512]{1,0:T(8,128)(2,1)}, bf16[256,512]{1,0:T(8,128)(2,1)}, u32[]{:S(2)}, u32[]{:S(2)}) collective-permute-start(bf16[256,512]{1,0:T(8,128)(2,1)} %get-tuple-element.4), channel_id=1, source_target_pairs={{0,1},{1,0},{2,3},{3,2},{4,5},{5,4},{6,7},{7,6},{8,9},{9,8},{10,11... | collective-permute-start | bytes 786440 | tf_op jit(solution)/shard_map/ppermute | solution.py:200
  11.3 14.8 %copy-start.5 = (bf16[256,512]{1,0:T(8,128)(2,1)S(1)}, bf16[256,512]{1,0:T(8,128)(2,1)}, u32[]{:S(2)}) copy-start(bf16[256,512]{1,0:T(8,128)(2,1)} %get-tuple-element.5) | copy-start | bytes 786436
  11.4 27.4 %collective-permute-start.12 = (bf16[512,512]{1,0:T(8,128)(2,1)S(1)}, bf16[512,512]{1,0:T(8,128)(2,1)S(1)}, u32[]{:S(2)}, u32[]{:S(2)}) collective-permute-start(bf16[512,512]{1,0:T(8,128)(2,1)S(1)} %dynamic-slice_bitcast_fusion), channel_id=1, source_target_pairs={{8,2},{9,3},{10,0},{11,1},{12,6},{13,7},{14,4},{15,5},{16,10},{17,... | collective-permute-start | bytes 1572872 | tf_op jit(solution)/shard_map/ppermute | solution.py:200
  21.7 17.8 %collective-permute-start.6 = (bf16[512,512]{1,0:T(8,128)(2,1)S(1)}, bf16[512,512]{1,0:T(8,128)(2,1)S(1)}, u32[]{:S(2)}, u32[]{:S(2)}) collective-permute-start(bf16[512,512]{1,0:T(8,128)(2,1)S(1)} %shard_map.72.a), channel_id=1, source_target_pairs={{0,2},{1,3},{6,4},{7,5},{8,10},{9,11},{14,12},{15,13},{16,18},{17,... | collective-permute-start | bytes 1572872 | tf_op jit(solution)/shard_map/ppermute | solution.py:200
  25.4 15.4 %collective-permute-start.13 = (bf16[512,512]{1,0:T(8,128)(2,1)S(1)}, bf16[512,512]{1,0:T(8,128)(2,1)S(1)}, u32[]{:S(2)}, u32[]{:S(2)}) collective-permute-start(bf16[512,512]{1,0:T(8,128)(2,1)S(1)} %dynamic-slice_bitcast_fusion), channel_id=1, source_target_pairs={{10,4},{11,5},{12,2},{13,3},{18,12},{19,13},{20,10},{21,11},{26,20... | collective-permute-start | bytes 1572872 | tf_op jit(solution)/shard_map/ppermute | solution.py:200
  26.1 9.2 %collective-permute-start.2 = (bf16[256,512]{1,0:T(8,128)(2,1)S(1)}, bf16[256,512]{1,0:T(8,128)(2,1)S(1)}, u32[]{:S(2)}, u32[]{:S(2)}) collective-permute-start(bf16[256,512]{1,0:T(8,128)(2,1)S(1)} %copy-done.5), channel_id=1, source_target_pairs={{0,1},{1,0},{2,3},{3,2},{4,5},{5,4},{6,7},{7,6},{8,9},{9,8},{10,11... | collective-permute-start | bytes 786440 | tf_op jit(solution)/shard_map/ppermute | solution.py:200
  28.3 16.2 %collective-permute-start.1 = (bf16[512,512]{1,0:T(8,128)(2,1)S(1)}, bf16[512,512]{1,0:T(8,128)(2,1)S(1)}, u32[]{:S(2)}, u32[]{:S(2)}) collective-permute-start(bf16[512,512]{1,0:T(8,128)(2,1)S(1)} %shard_map.69), channel_id=1, source_target_pairs={{0,1},{1,0},{2,3},{3,2},{4,5},{5,4},{6,7},{7,6},{8,9},{9,8},{10,11... | collective-permute-start | bytes 1572872 | tf_op jit(solution)/shard_map/ppermute | solution.py:200
  37.4 12.6 %collective-permute-start.3 = (bf16[512,512]{1,0:T(8,128)(2,1)S(1)}, bf16[512,512]{1,0:T(8,128)(2,1)S(1)}, u32[]{:S(2)}, u32[]{:S(2)}) collective-permute-start(bf16[512,512]{1,0:T(8,128)(2,1)S(1)} %shard_map.70.a), channel_id=1, source_target_pairs={{0,2},{1,3},{6,4},{7,5},{8,10},{9,11},{14,12},{15,13},{16,18},{17,... | collective-permute-start | bytes 1572872 | tf_op jit(solution)/shard_map/ppermute | solution.py:200
  38.7 12.5 %collective-permute-start.15 = (bf16[512,512]{1,0:T(8,128)(2,1)S(1)}, bf16[512,512]{1,0:T(8,128)(2,1)S(1)}, u32[]{:S(2)}, u32[]{:S(2)}) collective-permute-start(bf16[512,512]{1,0:T(8,128)(2,1)S(1)} %collective-permute-done.12.rest_1_.w1), channel_id=1, source_target_pairs={{2,4},{3,5},{4,2},{5,3},{10,12},{11,13},{12,10},{13,11},{18,20},{1... | collective-permute-start | bytes 1572872 | tf_op jit(solution)/shard_map/ppermute | solution.py:200
  40.1 13.1 %collective-permute-start.7 = (bf16[512,512]{1,0:T(8,128)(2,1)S(1)}, bf16[512,512]{1,0:T(8,128)(2,1)S(1)}, u32[]{:S(2)}, u32[]{:S(2)}) collective-permute-start(bf16[512,512]{1,0:T(8,128)(2,1)S(1)} %shard_map.73), channel_id=1, source_target_pairs={{2,4},{3,5},{4,2},{5,3},{10,12},{11,13},{12,10},{13,11},{18,20},{1... | collective-permute-start | bytes 1572872 | tf_op jit(solution)/shard_map/ppermute | solution.py:200
  40.8 15.1 %collective-permute-start.11 = (bf16[512,512]{1,0:T(8,128)(2,1)S(1)}, bf16[512,512]{1,0:T(8,128)(2,1)S(1)}, u32[]{:S(2)}, u32[]{:S(2)}) collective-permute-start(bf16[512,512]{1,0:T(8,128)(2,1)S(1)} %dynamic-slice_bitcast_fusion), channel_id=1, source_target_pairs={{8,0},{9,1},{10,2},{11,3},{12,4},{13,5},{14,6},{15,7},{16,8},{17,9... | collective-permute-start | bytes 1572872 | tf_op jit(solution)/shard_map/ppermute | solution.py:200
  44.5 27.1 %collective-permute-start.10 = (bf16[512,512]{1,0:T(8,128)(2,1)S(1)}, bf16[512,512]{1,0:T(8,128)(2,1)S(1)}, u32[]{:S(2)}, u32[]{:S(2)}) collective-permute-start(bf16[512,512]{1,0:T(8,128)(2,1)S(1)} %shard_map.77), channel_id=1, source_target_pairs={{8,0},{9,1},{10,2},{11,3},{12,4},{13,5},{14,6},{15,7},{16,8},{17,9... | collective-permute-start | bytes 1572872 | tf_op jit(solution)/shard_map/ppermute | solution.py:200
  50.0 24.2 %collective-permute-start.14 = (bf16[512,512]{1,0:T(8,128)(2,1)S(1)}, bf16[512,512]{1,0:T(8,128)(2,1)S(1)}, u32[]{:S(2)}, u32[]{:S(2)}) collective-permute-start(bf16[512,512]{1,0:T(8,128)(2,1)S(1)} %collective-permute-done.13.w2), channel_id=1, source_target_pairs={{2,0},{3,1},{4,6},{5,7},{10,8},{11,9},{12,14},{13,15},{18,16},{19,... | collective-permute-start | bytes 1572872 | tf_op jit(solution)/shard_map/ppermute | solution.py:200
  51.3 26.3 %collective-permute-start.16 = (bf16[512,512]{1,0:T(8,128)(2,1)S(1)}, bf16[512,512]{1,0:T(8,128)(2,1)S(1)}, u32[]{:S(2)}, u32[]{:S(2)}) collective-permute-start(bf16[512,512]{1,0:T(8,128)(2,1)S(1)} %collective-permute-done.15.w3), channel_id=1, source_target_pairs={{2,0},{3,1},{4,6},{5,7},{10,8},{11,9},{12,14},{13,15},{18,16},{19,... | collective-permute-start | bytes 1572872 | tf_op jit(solution)/shard_map/ppermute | solution.py:200
  53.2 26.9 %collective-permute-start.4 = (bf16[512,512]{1,0:T(8,128)(2,1)S(1)}, bf16[512,512]{1,0:T(8,128)(2,1)S(1)}, u32[]{:S(2)}, u32[]{:S(2)}) collective-permute-start(bf16[512,512]{1,0:T(8,128)(2,1)S(1)} %shard_map.71), channel_id=1, source_target_pairs={{2,4},{3,5},{4,2},{5,3},{10,12},{11,13},{12,10},{13,11},{18,20},{1... | collective-permute-start | bytes 1572872 | tf_op jit(solution)/shard_map/ppermute | solution.py:200
  56.0 32.8 %collective-permute-start.8 = (bf16[512,512]{1,0:T(8,128)(2,1)S(1)}, bf16[512,512]{1,0:T(8,128)(2,1)S(1)}, u32[]{:S(2)}, u32[]{:S(2)}) collective-permute-start(bf16[512,512]{1,0:T(8,128)(2,1)S(1)} %shard_map.74), channel_id=1, source_target_pairs={{0,2},{1,3},{2,0},{3,1},{4,6},{5,7},{6,4},{7,5},{8,10},{9,11},{10,... | collective-permute-start | bytes 1572872 | tf_op jit(solution)/shard_map/ppermute | solution.py:200
  72.6 19.9 %collective-permute-start.17 = (bf16[256,1024]{1,0:T(8,128)(2,1)S(1)}, bf16[256,1024]{1,0:T(8,128)(2,1)S(1)}, u32[]{:S(2)}, u32[]{:S(2)}) collective-permute-start(bf16[256,1024]{1,0:T(8,128)(2,1)S(1)} %shard_map.78), channel_id=1, source_target_pairs={{0,1},{1,0},{2,3},{3,2},{4,5},{5,4},{6,7},{7,6},{8,9},{9,8},{10,11... | collective-permute-start | bytes 1572872 | tf_op jit(solution)/shard_map/ppermute | solution.py:200
  78.6 20.1 %collective-permute-start.18 = (bf16[256,1024]{1,0:T(8,128)(2,1)S(1)}, bf16[256,1024]{1,0:T(8,128)(2,1)S(1)}, u32[]{:S(2)}, u32[]{:S(2)}) collective-permute-start(bf16[256,1024]{1,0:T(8,128)(2,1)S(1)} %shard_map.79), channel_id=1, source_target_pairs={{0,1},{1,0},{2,3},{3,2},{4,5},{5,4},{6,7},{7,6},{8,9},{9,8},{10,11... | collective-permute-start | bytes 1572872 | tf_op jit(solution)/shard_map/ppermute | solution.py:200
  90.8 17.2 %collective-permute-start.9 = (bf16[512,512]{1,0:T(8,128)(2,1)S(1)}, bf16[512,512]{1,0:T(8,128)(2,1)S(1)}, u32[]{:S(2)}, u32[]{:S(2)}) collective-permute-start(bf16[512,512]{1,0:T(8,128)(2,1)S(1)} %shard_map.75.mine), channel_id=1, source_target_pairs={{0,1},{1,0},{2,3},{3,2},{4,5},{5,4},{6,7},{7,6},{8,9},{9,8},{10,11... | collective-permute-start | bytes 1572872 | tf_op jit(solution)/shard_map/ppermute | solution.py:200
  (1 other events, 0.7 us)

commit v2 on v1

--- a/solution.py
+++ b/solution.py
@@ -10,6 +10,8 @@
 
 
 HEAD = 128
+PARTS = 2
+SHARE = 4
 AXES = ("section", "shard", "replica")
 BF16 = jnp.bfloat16
 F32 = jnp.float32
@@ -75,6 +77,10 @@
     blocks = blocks or {}
     nbytes = sum(a.size * a.dtype.itemsize for i, a in enumerate(args) if i not in blocks)
     in_specs = [blocks.get(i, spec) for i in range(len(args))]
+    return kernel_call(body, out_shape, ids, args, in_specs, place, aliases, scratch, grant, flops, nbytes, spec)
+
+
+def kernel_call(body, out_shape, ids, args, in_specs, place, aliases, scratch, grant, flops, nbytes, spec):
     whole = place or pl.BlockSpec(out_shape.shape, lambda i, ids: (0,) * len(out_shape.shape))
     in_specs = [
         pl.BlockSpec(a.shape, lambda i, ids, n=len(a.shape): (0,) * n) if s is spec else s
@@ -131,13 +137,14 @@
     return lax.dot_general(keys, rows, (((1,), (1,)), ((), ())), preferred_element_type=F32)
 
 
-def term_body(slot, place, ids, normed, ours, theirs, other, *rest):
+def term_body(slot, at, place, ids, normed, ours, theirs, other, *rest):
     *sums, out, rows, sem = rest
-    count, half = rows.shape
-    cols = pl.ds(pl.multiple_of(ids[slot] * half, half), half)
+    count, size = rows.shape
+    half = other.shape[1]
+    cols = pl.ds(pl.multiple_of(ids[slot] * half + at, size), size)
     fetch = pltpu.make_async_copy(normed.at[:, cols], rows, sem)
     fetch.start()
-    total = outer(other[pl.ds(place * count, count), :], theirs[...])
+    total = outer(other[pl.ds(place * count, count), pl.ds(at, size)], theirs[...])
     fetch.wait()
     total = total + outer(rows[...], ours[...])
     for part in sums:
@@ -145,39 +152,48 @@
     out[...] = total.astype(out.dtype)
 
 
+def own_share(ids, block, share):
+    skip = pl.multiple_of(ids[8] * (block.shape[0] - share), HEAD)
+    return pl.ds(skip, share)
+
+
 def share_body(ids, keys, *rest):
     *blocks, out = rest
-    count, half = out.shape[0], blocks[0].shape[0]
+    count, share = out.shape[0], out.shape[1] // len(blocks)
     for i, block in enumerate(blocks):
-        part = inner(keys[pl.ds(count, count), :], block[...])
-        out[:, pl.ds(i * half, half)] = part.astype(out.dtype)
-
-
-def share_pair_body(ids, keys, w2, w4, w3, w5, out):
-    count, half = out.shape[0], w2.shape[0]
-    for i, (near, far) in enumerate(((w2, w4), (w3, w5))):
-        part = inner(keys[pl.ds(count, count), :], near[...] + far[...])
-        out[:, pl.ds(i * half, half)] = part.astype(out.dtype)
-
-
-def passed_body(ids, keys, w0, w1, w2, w4, w3, w5, near, far, out):
-    count, half = out.shape[0], w0.shape[0]
+        part = inner(keys[pl.ds(count, count), :], block[own_share(ids, block, share), :])
+        out[:, pl.ds(i * share, share)] = part.astype(out.dtype)
+
+
+def share_pair_body(ids, keys, one, two, out):
+    count, share = out.shape
+    mine = own_share(ids, one, share)
+    part = inner(keys[pl.ds(count, count), :], one[mine, :] + two[mine, :])
+    out[...] = part.astype(out.dtype)
+
+
+def passed_body(ids, keys, w0, w1, w2, w4, w3, w5, near, mid, far, out):
+    count, held, share = out.shape[0], w0.shape[0], mid.shape[1]
     for i in range(4):
         block = (w0, w1)[i][...] if i < 2 else (w2, w3)[i - 2][...] + (w4, w5)[i - 2][...]
-        mine = pl.multiple_of(ids[i] * half, half)
-        theirs = pl.multiple_of(ids[4 + i] * half, half)
-        out[:, pl.ds(mine, half)] = inner(keys[pl.ds(0, count), :], block).astype(out.dtype)
-        out[:, pl.ds(theirs, half)] = (near, far)[i // 2][:, pl.ds(i % 2 * half, half)]
+        base = lax.div(ids[i] - ids[8], 2) * (held + share)
+        mine = pl.multiple_of(base + ids[8] * share, HEAD)
+        theirs = pl.multiple_of(base + (1 - ids[8]) * held, HEAD)
+        out[:, pl.ds(mine, held)] = inner(keys[pl.ds(0, count), :], block).astype(out.dtype)
+        out[:, pl.ds(theirs, share)] = near[:, pl.ds(i * share, share)] if i < 2 else (mid, far)[i - 2][...]
 
 
 def add_body(ids, a, b, out):
     out[...] = (a[...].astype(F32) + b[...].astype(F32)).astype(out.dtype)
 
 
-def rows_body(ids, mine, theirs, out):
-    half = mine.shape[0]
-    out[pl.ds(pl.multiple_of(ids[8] * half, half), half), :] = mine[...]
-    out[pl.ds(pl.multiple_of((1 - ids[8]) * half, half), half), :] = theirs[...]
+def rows_body(ids, *refs):
+    *parts, out = refs
+    count, size = len(parts) // 2, parts[0].shape[0]
+    for i, part in enumerate(parts):
+        half = ids[8] if i < count else 1 - ids[8]
+        at = pl.multiple_of((half * count + i % count) * size, size)
+        out[pl.ds(at, size), :] = part[...]
 
 
 def pair_device(normed, key_cotangent, positions, key_weight):
@@ -187,11 +203,12 @@
     count = micro * tokens
     depth = key_cotangent.shape[-1]
     half = key_weight.shape[1] // replicas
+    share = key_weight.shape[1] * SHARE // 8
     out = lambda *shape: jax.ShapeDtypeStruct(shape, BF16)
 
-    def send(value, line, back=0, swap=0):
+    def send(value, line, back=0, swap=0, drop=0):
         pairs = []
-        for a in range(back, sections):
+        for a in range(back, sections - drop):
             for b in range(shards):
                 for c in range(replicas):
                     if line(b) is not None:
@@ -219,7 +236,7 @@
     ours = call(rotate_body, out(count, depth), ids, freq, positions,
                 key_cotangent.reshape(count, depth))
     theirs = send(ours, stay, swap=1)
-    piece = lax.dynamic_slice(key_weight[0], (y * half, 0), (half, depth))
+    piece = lax.dynamic_slice(key_weight[0], (y * share, 0), (replicas * half - share, depth))
     w1 = send(piece, flip, back=1)
     w2 = send(piece, across, back=1)
     w0 = send(piece, stay, back=1)
@@ -229,38 +246,48 @@
                  blocks={0: block_of(flat, half, 5), 1: block_of(flat, half, 4)})
     other2 = send(pack2, stay, swap=1)
 
-    def term(slot, place, other, *sums):
-        return call(functools.partial(term_body, slot, place), out(half, depth), ids,
-                    flat, ours, theirs, other, *sums, blocks={0: pl.BlockSpec(memory_space=pltpu.HBM)},
-                    scratch=[pltpu.VMEM((count, half), BF16), pltpu.SemaphoreType.DMA],
-                    flops=4 * count * half * depth)
+    def term(slot, place, other, *sums, part=0, parts=1, blocks=None):
+        size = half // parts
+        return call(functools.partial(term_body, slot, part * size, place), out(size, depth), ids,
+                    flat, ours, theirs, other, *sums,
+                    blocks={0: pl.BlockSpec(memory_space=pltpu.HBM)} | (blocks or {}),
+                    scratch=[pltpu.VMEM((count, size), BF16), pltpu.SemaphoreType.DMA],
+                    flops=4 * count * size * depth)
 
     def plus(a, b):
-        return call(add_body, out(half, depth), ids, a, b)
-
+        return call(add_body, out(*a.shape), ids, a, b)
+
+    cut = range(PARTS)
+    part_of = lambda i: pl.BlockSpec((half // PARTS, depth), lambda n, ids: (i, 0))
     term3 = term(3, 0, other0)
     a1 = send(term3, inward)
-    w3 = send(w1, across)
-    w4 = send(w2, outward)
+    w3 = send(w1, across, drop=1)
+    w4 = send(w2, outward, drop=1)
     both = call(copy_body, out(2 * count, depth), ids, ours, theirs)
     keys = send(both, stay, back=1)
     term2 = term(2, 0, other1)
     a2 = send(term2, inward)
     b1 = send(plus(term3, a1), across)
-    w5 = send(w3, outward)
+    w5 = send(w3, outward, drop=1)
     b2 = send(plus(term2, a2), across)
-    c1 = send(term(1, 0, other2, b1), flip)
-    near = call(share_body, out(count, 2 * half), ids, keys, w0, w1,
-                flops=4 * count * half * depth)
+    term1 = [term(1, 0, other2, b1, part=i, parts=PARTS, blocks={4: part_of(i)}) for i in cut]
+    c1 = [send(term1[i], flip) for i in cut]
+    near = call(share_body, out(count, 2 * share), ids, keys, w0, w1,
+                flops=4 * count * share * depth)
     near = send(near, stay, swap=1)
-    far = call(share_pair_body, out(count, 2 * half), ids, keys, w2, w4, w3, w5,
-               flops=4 * count * half * depth)
+    mid = call(share_pair_body, out(count, share), ids, keys, w2, w4, flops=2 * count * share * depth)
+    mid = send(mid, stay, swap=1)
+    far = call(share_pair_body, out(count, share), ids, keys, w3, w5, flops=2 * count * share * depth)
     far = send(far, stay, swap=1)
-    mine = term(0, 1, other2, b2, c1)
-    rest = send(mine, stay, swap=1)
-    passed = call(passed_body, out(count, width), ids, keys, w0, w1, w2, w4, w3, w5, near, far,
-                  flops=8 * count * half * depth)
-    weight_grad = call(rows_body, out(replicas * half, depth), ids, mine, rest)
+    mine = [
+        term(0, 1, other2, c1[i], b2, part=i, parts=PARTS,
+             blocks={5: part_of(i)})
+        for i in cut
+    ]
+    rest = [send(mine[i], stay, swap=1) for i in cut]
+    passed = call(passed_body, out(count, width), ids, keys, w0, w1, w2, w4, w3, w5, near, mid, far,
+                  flops=2 * count * width * depth)
+    weight_grad = call(rows_body, out(replicas * half, depth), ids, *mine, *rest)
     return weight_grad[None], passed.reshape(normed.shape)
 
 

time: 110 us -> 97.6 us (0.89)
  waiting for transfers between devices: 43.4 us -> 33.6 us
  starting transfers between devices: 39.9 us -> 32.8 us
  Pallas kernels: 19 us -> 23.2 us
    ppermute x19 -> x22, waiting for transfers between devices: 43.4 us -> 33.6 us  [send(): return lax.ppermute(value, AXES, pairs)]
    ppermute x19 -> x22, starting transfers between devices: 39.9 us -> 32.8 us  [send(): return lax.ppermute(value, AXES, pairs)]
    pallas_call x13 -> x16, Pallas kernels: 19 us -> 23.2 us  [kernel_call(): pl.pallas_call(body, out_shape=out_shape, grid_spec=pltpu.PrefetchScalarG...]
    unnamed x12 -> x10, local copies, waits for them, and re-layouts: 2.46 us -> 2.45 us
  transfers between devices with their start and end apart: 19 -> 22, of which waited for: 9 -> 9; matrix products, arithmetic and copies ran while one was open for 2% -> 3% of each run, Pallas kernels for 15% -> 21%
where the time goes in v2:
time: 97.6 us; the launch traced here: 97 us
  waiting for transfers between devices  33.6 us (34%)
  starting transfers between devices  32.8 us (34%)
  Pallas kernels  23.2 us (24%)
  local copies, waits for them, and re-layouts  4.93 us (5%)
  between operations  2.25 us (2%)
    ppermute x22, waiting for transfers between devices, send(): return lax.ppermute(value, AXES, pairs)  33.6 us
    ppermute x22, starting transfers between devices, send(): return lax.ppermute(value, AXES, pairs)  32.8 us
    pallas_call x16, Pallas kernels, kernel_call(): pl.pallas_call(body, out_shape=out_shape, grid_spec=pltpu.PrefetchScalarG...  23.2 us
    unnamed x10, local copies, waits for them, and re-layouts  2.45 us
  transfers between devices with their start and end apart: 22, of which 9 were waited for; matrix products, arithmetic and copies ran while one was open for 3% of the time, Pallas kernels for 21%

profile of v2, /device:TPU:0, one launch (start us, length us, event | category | flops | bytes accessed | tf_op | source)
XLA Modules:
  0.0 97.0 jit_solution(16938016344606514860)
XLA Ops:
  4.5 3.1 %collective-permute-start = (bf16[256,512]{1,0:T(8,128)(2,1)S(1)}, bf16[256,512]{1,0:T(8,128)(2,1)}, u32[]{:S(2)}, u32[]{:S(2)}) collective-permute-start(bf16[256,512]{1,0:T(8,128)(2,1)S(1)} %shard_map.68.ours.refs_0_), channel_id=1, source_target_pairs={{0,1},{1,0},{2,3},{3,2},{4,5},{5,4},{6,7},{7,6},{8,9},{9,8},{10,11... | collective-permute-start | bytes 786440 | tf_op jit(solution)/shard_map/ppermute | solution.py:217
  9.4 1.9 %constant_dynamic-slice_fusion = (bf16[256,512]{1,0:T(8,128)(2,1)}, bf16[256,512]{1,0:T(8,128)(2,1)}) fusion(bf16[256,4096]{1,0:T(8,128)(2,1)} %bitcast.13, s32[]{:T(128)S(6)} %select_n.15, s32[]{:T(128)S(6)} %select_n.14), kind=kLoop, calls=%fused_computation.1 | loop fusion | bytes 1048584 | tf_op jit(solution)/shard_map/dynamic_slice | solution.py:243
  13.4 2.1 %collective-permute-start.6 = (bf16[256,512]{1,0:T(8,128)(2,1)}, bf16[256,512]{1,0:T(8,128)(2,1)S(1)}, u32[]{:S(2)}, u32[]{:S(2)}) collective-permute-start(bf16[256,512]{1,0:T(8,128)(2,1)} %get-tuple-element.4), channel_id=1, source_target_pairs={{0,1},{1,0},{2,3},{3,2},{4,5},{5,4},{6,7},{7,6},{8,9},{9,8},{10,11... | collective-permute-start | bytes 786440 | tf_op jit(solution)/shard_map/ppermute | solution.py:217
  15.4 4.6 %collective-permute-done.2.other = bf16[256,512]{1,0:T(8,128)(2,1)} collective-permute-done((bf16[256,512]{1,0:T(8,128)(2,1)}, bf16[256,512]{1,0:T(8,128)(2,1)}, u32[]{:S(2)}, u32[]{:S(2)}) %collective-permute-start.2) | collective-permute-done | bytes 262176 | tf_op jit(solution)/shard_map/ppermute | solution.py:217
  20.0 2.1 %shard_map.70.a = bf16[512,512]{1,0:T(8,128)(2,1)S(1)} custom-call(s32[10]{0:T(128)S(1)} %pad_add_fusion.ids, bf16[256,4096]{1,0:T(8,128)(2,1)S(1)} %bitcast.14, bf16[256,512]{1,0:T(8,128)(2,1)S(1)} %shard_map.68.ours.refs_0_, bf16[256,512]{1,0:T(8,128)(2,1)} %collective-permute-done.theirs.refs_1_, bf16[256,512]{1,0:T(8,128)(2,1)} %collective-permute-done.2.other), custom_call_target="tpu_custom_call" | custom-call | flops 268435456 | bytes 786432 | tf_op jit(solution)/shard_map/pallas_call | solution.py:89
  22.1 3.4 %collective-permute-start.3 = (bf16[512,512]{1,0:T(8,128)(2,1)S(1)}, bf16[512,512]{1,0:T(8,128)(2,1)S(1)}, u32[]{:S(2)}, u32[]{:S(2)}) collective-permute-start(bf16[512,512]{1,0:T(8,128)(2,1)S(1)} %shard_map.70.a), channel_id=1, source_target_pairs={{0,2},{1,3},{6,4},{7,5},{8,10},{9,11},{14,12},{15,13},{16,18},{17,... | collective-permute-start | bytes 1572872 | tf_op jit(solution)/shard_map/ppermute | solution.py:217
  26.8 2.0 %shard_map.73.a = bf16[512,512]{1,0:T(8,128)(2,1)S(1)} custom-call(s32[10]{0:T(128)S(1)} %pad_add_fusion.ids, bf16[256,4096]{1,0:T(8,128)(2,1)S(1)} %bitcast.15, bf16[256,512]{1,0:T(8,128)(2,1)S(1)} %shard_map.68.ours.refs_0_, bf16[256,512]{1,0:T(8,128)(2,1)} %collective-permute-done.theirs.refs_1_, bf16[256,512]{1,0:T(8,128)(2,1)S(1)} %collective-permute-done.6.other), custom_call_target="tpu_custom_call" | custom-call | flops 268435456 | bytes 786432 | tf_op jit(solution)/shard_map/pallas_call | solution.py:89
  28.8 2.0 %collective-permute-start.7 = (bf16[512,512]{1,0:T(8,128)(2,1)S(1)}, bf16[512,512]{1,0:T(8,128)(2,1)S(1)}, u32[]{:S(2)}, u32[]{:S(2)}) collective-permute-start(bf16[512,512]{1,0:T(8,128)(2,1)S(1)} %shard_map.73.a), channel_id=1, source_target_pairs={{0,2},{1,3},{6,4},{7,5},{8,10},{9,11},{14,12},{15,13},{16,18},{17,... | collective-permute-start | bytes 1572872 | tf_op jit(solution)/shard_map/ppermute | solution.py:217
  31.6 1.5 %shard_map.79 = bf16[512,512]{1,0:T(8,128)(2,1)S(1)} custom-call(s32[10]{0:T(128)S(1)} %pad_add_fusion.ids, bf16[256,512]{1,0:T(8,128)(2,1)S(1)} %shard_map.68.ours.refs_0_, bf16[256,512]{1,0:T(8,128)(2,1)} %collective-permute-done.theirs.refs_1_), custom_call_target="tpu_custom_call" | custom-call | bytes 524288 | tf_op jit(solution)/shard_map/pallas_call | solution.py:89
  35.0 2.8 %collective-permute-done.3.b = bf16[512,512]{1,0:T(8,128)(2,1)S(1)} collective-permute-done((bf16[512,512]{1,0:T(8,128)(2,1)S(1)}, bf16[512,512]{1,0:T(8,128)(2,1)S(1)}, u32[]{:S(2)}, u32[]{:S(2)}) %collective-permute-start.3) | collective-permute-done | bytes 524320 | tf_op jit(solution)/shard_map/ppermute | solution.py:217
  37.7 1.5 %collective-permute-start.1 = (bf16[512,512]{1,0:T(8,128)(2,1)S(1)}, bf16[512,512]{1,0:T(8,128)(2,1)S(1)}, u32[]{:S(2)}, u32[]{:S(2)}) collective-permute-start(bf16[512,512]{1,0:T(8,128)(2,1)S(1)} %shard_map.69), channel_id=1, source_target_pairs={{0,1},{1,0},{2,3},{3,2},{4,5},{5,4},{6,7},{7,6},{8,9},{9,8},{10,11... | collective-permute-start | bytes 1572872 | tf_op jit(solution)/shard_map/ppermute | solution.py:217
  40.6 6.4 %collective-permute-done.7.b = bf16[512,512]{1,0:T(8,128)(2,1)S(1)} collective-permute-done((bf16[512,512]{1,0:T(8,128)(2,1)S(1)}, bf16[512,512]{1,0:T(8,128)(2,1)S(1)}, u32[]{:S(2)}, u32[]{:S(2)}) %collective-permute-start.7) | collective-permute-done | bytes 524320 | tf_op jit(solution)/shard_map/ppermute | solution.py:217
  53.5 1.9 %shard_map.76 = bf16[256,512]{1,0:T(8,128)(2,1)S(1)} custom-call(s32[10]{0:T(128)S(1)} %pad_add_fusion.ids, bf16[256,4096]{1,0:T(8,128)(2,1)S(1)} %bitcast.18, bf16[256,512]{1,0:T(8,128)(2,1)S(1)} %shard_map.68.ours.refs_0_, bf16[256,512]{1,0:T(8,128)(2,1)} %collective-permute-done.theirs.refs_1_, bf16[512,512]{1,0:T(8,128)(2,1)S(1)} %collective-permute-done.1.other, ...), custom_call_target="tpu_custom_call" | custom-call | flops 134217728 | bytes 1048576 | tf_op jit(solution)/shard_map/pallas_call | solution.py:89
  55.4 5.7 %collective-permute-start.9 = (bf16[256,512]{1,0:T(8,128)(2,1)S(1)}, bf16[256,512]{1,0:T(8,128)(2,1)S(1)}, u32[]{:S(2)}, u32[]{:S(2)}) collective-permute-start(bf16[256,512]{1,0:T(8,128)(2,1)S(1)} %shard_map.76), channel_id=1, source_target_pairs={{0,2},{1,3},{2,0},{3,1},{4,6},{5,7},{6,4},{7,5},{8,10},{9,11},{10,... | collective-permute-start | bytes 786440 | tf_op jit(solution)/shard_map/ppermute | solution.py:217
  61.1 1.9 %shard_map.72 = bf16[256,512]{1,0:T(8,128)(2,1)S(1)} custom-call(s32[10]{0:T(128)S(1)} %pad_add_fusion.ids, bf16[256,4096]{1,0:T(8,128)(2,1)S(1)} %bitcast.19, bf16[256,512]{1,0:T(8,128)(2,1)S(1)} %shard_map.68.ours.refs_0_, bf16[256,512]{1,0:T(8,128)(2,1)} %collective-permute-done.theirs.refs_1_, bf16[512,512]{1,0:T(8,128)(2,1)S(1)} %collective-permute-done.1.other, ...), custom_call_target="tpu_custom_call" | custom-call | flops 134217728 | bytes 1048576 | tf_op jit(solution)/shard_map/pallas_call | solution.py:89
  64.6 10.3 %collective-permute-done.18.two.w5 = bf16[512,512]{1,0:T(8,128)(2,1)S(1)} collective-permute-done((bf16[512,512]{1,0:T(8,128)(2,1)S(1)}, bf16[512,512]{1,0:T(8,128)(2,1)S(1)}, u32[]{:S(2)}, u32[]{:S(2)}) %collective-permute-start.18) | collective-permute-done | bytes 524320 | tf_op jit(solution)/shard_map/ppermute | solution.py:217
  78.0 2.6 %collective-permute-done.9.rest_0_ = bf16[256,512]{1,0:T(8,128)(2,1)S(1)} collective-permute-done((bf16[256,512]{1,0:T(8,128)(2,1)S(1)}, bf16[256,512]{1,0:T(8,128)(2,1)S(1)}, u32[]{:S(2)}, u32[]{:S(2)}) %collective-permute-start.9) | collective-permute-done | bytes 262176 | tf_op jit(solution)/shard_map/ppermute | solution.py:217
  80.6 1.9 %shard_map.77.refs_1_ = bf16[256,512]{1,0:T(8,128)(2,1)S(1)} custom-call(s32[10]{0:T(128)S(1)} %pad_add_fusion.ids, bf16[256,4096]{1,0:T(8,128)(2,1)S(1)} %bitcast.20, bf16[256,512]{1,0:T(8,128)(2,1)S(1)} %shard_map.68.ours.refs_0_, bf16[256,512]{1,0:T(8,128)(2,1)} %collective-permute-done.theirs.refs_1_, bf16[512,512]{1,0:T(8,128)(2,1)S(1)} %collective-permute-done.1.other, ...), custom_call_target="tpu_custom_call" | custom-call | flops 134217728 | bytes 1310720 | tf_op jit(solution)/shard_map/pallas_call | solution.py:89
  83.9 1.9 %shard_map.75.refs_0_ = bf16[256,512]{1,0:T(8,128)(2,1)S(1)} custom-call(s32[10]{0:T(128)S(1)} %pad_add_fusion.ids, bf16[256,4096]{1,0:T(8,128)(2,1)S(1)} %bitcast.21, bf16[256,512]{1,0:T(8,128)(2,1)S(1)} %shard_map.68.ours.refs_0_, bf16[256,512]{1,0:T(8,128)(2,1)} %collective-permute-done.theirs.refs_1_, bf16[512,512]{1,0:T(8,128)(2,1)S(1)} %collective-permute-done.1.other, ...), custom_call_target="tpu_custom_call" | custom-call | flops 134217728 | bytes 1310720 | tf_op jit(solution)/shard_map/pallas_call | solution.py:89
  86.8 1.6 %collective-permute-done.21.far = bf16[256,512]{1,0:T(8,128)(2,1)S(1)} collective-permute-done((bf16[256,512]{1,0:T(8,128)(2,1)S(1)}, bf16[256,512]{1,0:T(8,128)(2,1)S(1)}, u32[]{:S(2)}, u32[]{:S(2)}) %collective-permute-start.21) | collective-permute-done | bytes 262176 | tf_op jit(solution)/shard_map/ppermute | solution.py:217
  88.4 2.6 %shard_map.83 = bf16[256,4096]{1,0:T(8,128)(2,1)} custom-call(s32[10]{0:T(128)S(1)} %pad_add_fusion.ids, bf16[512,512]{1,0:T(8,128)(2,1)S(1)} %collective-permute-done.12.keys, bf16[512,512]{1,0:T(8,128)(2,1)S(1)} %collective-permute-done.13.rest_0_.w0, bf16[512,512]{1,0:T(8,128)(2,1)S(1)} %collective-permute-done.14.rest_1_.w1, ...), custom_call_target="tpu_custom_call" | custom-call | flops 1073741824 | bytes 4718592 | tf_op jit(solution)/shard_map/pallas_call | solution.py:89
  91.0 1.6 %collective-permute-done.11.refs_3_ = bf16[256,512]{1,0:T(8,128)(2,1)S(1)} collective-permute-done((bf16[256,512]{1,0:T(8,128)(2,1)S(1)}, bf16[256,512]{1,0:T(8,128)(2,1)S(1)}, u32[]{:S(2)}, u32[]{:S(2)}) %collective-permute-start.11) | collective-permute-done | bytes 262176 | tf_op jit(solution)/shard_map/ppermute | solution.py:217
  92.6 2.8 %collective-permute-done.10.refs_2_ = bf16[256,512]{1,0:T(8,128)(2,1)S(1)} collective-permute-done((bf16[256,512]{1,0:T(8,128)(2,1)S(1)}, bf16[256,512]{1,0:T(8,128)(2,1)S(1)}, u32[]{:S(2)}, u32[]{:S(2)}) %collective-permute-start.10) | collective-permute-done | bytes 262176 | tf_op jit(solution)/shard_map/ppermute | solution.py:217
  95.4 1.6 %shard_map.78 = bf16[1024,512]{1,0:T(8,128)(2,1)} custom-call(s32[10]{0:T(128)S(1)} %pad_add_fusion.ids, bf16[256,512]{1,0:T(8,128)(2,1)S(1)} %shard_map.75.refs_0_, bf16[256,512]{1,0:T(8,128)(2,1)S(1)} %shard_map.77.refs_1_, bf16[256,512]{1,0:T(8,128)(2,1)S(1)} %collective-permute-done.10.refs_2_, bf16[256,512]{1,0:T(8,128)(2,1)S(1)} %collective-permute-done.11.refs_3_), custom_call_target="tpu_custom_call" | custom-call | bytes 1048576 | tf_op jit(solution)/shard_map/pallas_call | solution.py:89
  (52 shorter events, 25.1 us)
Async XLA Ops:
  0.6 10.7 %copy-start = (bf16[1,1024,512]{2,1,0:T(8,128)(2,1)S(1)}, bf16[1,1024,512]{2,1,0:T(8,128)(2,1)}, u32[]{:S(2)}) copy-start(bf16[1,1024,512]{2,1,0:T(8,128)(2,1)} %param.8) | copy-start | bytes 3145732
  0.6 19.4 %copy-start.1 = (bf16[1,2,128,4096]{3,2,1,0:T(8,128)(2,1)S(1)}, bf16[1,2,128,4096]{3,2,1,0:T(8,128)(2,1)}, u32[]{:S(2)}) copy-start(bf16[1,2,128,4096]{3,2,1,0:T(8,128)(2,1)} %param.5) | copy-start | bytes 6291460
  4.5 11.0 %collective-permute-start = (bf16[256,512]{1,0:T(8,128)(2,1)S(1)}, bf16[256,512]{1,0:T(8,128)(2,1)}, u32[]{:S(2)}, u32[]{:S(2)}) collective-permute-start(bf16[256,512]{1,0:T(8,128)(2,1)S(1)} %shard_map.68.ours.refs_0_), channel_id=1, source_target_pairs={{0,1},{1,0},{2,3},{3,2},{4,5},{5,4},{6,7},{7,6},{8,9},{9,8},{10,11... | collective-permute-start | bytes 786440 | tf_op jit(solution)/shard_map/ppermute | solution.py:217
  11.3 8.7 %collective-permute-start.2 = (bf16[256,512]{1,0:T(8,128)(2,1)}, bf16[256,512]{1,0:T(8,128)(2,1)}, u32[]{:S(2)}, u32[]{:S(2)}) collective-permute-start(bf16[256,512]{1,0:T(8,128)(2,1)} %get-tuple-element.5), channel_id=1, source_target_pairs={{0,1},{1,0},{2,3},{3,2},{4,5},{5,4},{6,7},{7,6},{8,9},{9,8},{10,11... | collective-permute-start | bytes 786440 | tf_op jit(solution)/shard_map/ppermute | solution.py:217
  11.3 19.5 %collective-permute-start.14 = (bf16[512,512]{1,0:T(8,128)(2,1)S(1)}, bf16[512,512]{1,0:T(8,128)(2,1)S(1)}, u32[]{:S(2)}, u32[]{:S(2)}) collective-permute-start(bf16[512,512]{1,0:T(8,128)(2,1)S(1)} %dynamic-slice_bitcast_fusion), channel_id=1, source_target_pairs={{8,2},{9,3},{10,0},{11,1},{12,6},{13,7},{14,4},{15,5},{16,10},{17,... | collective-permute-start | bytes 1572872 | tf_op jit(solution)/shard_map/ppermute | solution.py:217
  12.7 20.4 %collective-permute-start.15 = (bf16[512,512]{1,0:T(8,128)(2,1)S(1)}, bf16[512,512]{1,0:T(8,128)(2,1)S(1)}, u32[]{:S(2)}, u32[]{:S(2)}) collective-permute-start(bf16[512,512]{1,0:T(8,128)(2,1)S(1)} %dynamic-slice_bitcast_fusion), channel_id=1, source_target_pairs={{10,4},{11,5},{12,2},{13,3},{18,12},{19,13},{20,10},{21,11},{26,20... | collective-permute-start | bytes 1572872 | tf_op jit(solution)/shard_map/ppermute | solution.py:217
  13.4 13.4 %collective-permute-start.6 = (bf16[256,512]{1,0:T(8,128)(2,1)}, bf16[256,512]{1,0:T(8,128)(2,1)S(1)}, u32[]{:S(2)}, u32[]{:S(2)}) collective-permute-start(bf16[256,512]{1,0:T(8,128)(2,1)} %get-tuple-element.4), channel_id=1, source_target_pairs={{0,1},{1,0},{2,3},{3,2},{4,5},{5,4},{6,7},{7,6},{8,9},{9,8},{10,11... | collective-permute-start | bytes 786440 | tf_op jit(solution)/shard_map/ppermute | solution.py:217
  22.1 15.6 %collective-permute-start.3 = (bf16[512,512]{1,0:T(8,128)(2,1)S(1)}, bf16[512,512]{1,0:T(8,128)(2,1)S(1)}, u32[]{:S(2)}, u32[]{:S(2)}) collective-permute-start(bf16[512,512]{1,0:T(8,128)(2,1)S(1)} %shard_map.70.a), channel_id=1, source_target_pairs={{0,2},{1,3},{6,4},{7,5},{8,10},{9,11},{14,12},{15,13},{16,18},{17,... | collective-permute-start | bytes 1572872 | tf_op jit(solution)/shard_map/ppermute | solution.py:217
  25.5 14.5 %collective-permute-start.13 = (bf16[512,512]{1,0:T(8,128)(2,1)S(1)}, bf16[512,512]{1,0:T(8,128)(2,1)S(1)}, u32[]{:S(2)}, u32[]{:S(2)}) collective-permute-start(bf16[512,512]{1,0:T(8,128)(2,1)S(1)} %dynamic-slice_bitcast_fusion), channel_id=1, source_target_pairs={{8,0},{9,1},{10,2},{11,3},{12,4},{13,5},{14,6},{15,7},{16,8},{17,9... | collective-permute-start | bytes 1572872 | tf_op jit(solution)/shard_map/ppermute | solution.py:217
  28.8 18.2 %collective-permute-start.7 = (bf16[512,512]{1,0:T(8,128)(2,1)S(1)}, bf16[512,512]{1,0:T(8,128)(2,1)S(1)}, u32[]{:S(2)}, u32[]{:S(2)}) collective-permute-start(bf16[512,512]{1,0:T(8,128)(2,1)S(1)} %shard_map.73.a), channel_id=1, source_target_pairs={{0,2},{1,3},{6,4},{7,5},{8,10},{9,11},{14,12},{15,13},{16,18},{17,... | collective-permute-start | bytes 1572872 | tf_op jit(solution)/shard_map/ppermute | solution.py:217
  30.9 17.5 %collective-permute-start.17 = (bf16[512,512]{1,0:T(8,128)(2,1)S(1)}, bf16[512,512]{1,0:T(8,128)(2,1)S(1)}, u32[]{:S(2)}, u32[]{:S(2)}) collective-permute-start(bf16[512,512]{1,0:T(8,128)(2,1)S(1)} %collective-permute-done.14.rest_1_.w1), channel_id=1, source_target_pairs={{2,4},{3,5},{4,2},{5,3},{10,12},{11,13},{12,10},{13,11},{18,20},{1... | collective-permute-start | bytes 1572872 | tf_op jit(solution)/shard_map/ppermute | solution.py:217
  33.1 17.2 %collective-permute-start.12 = (bf16[512,512]{1,0:T(8,128)(2,1)S(1)}, bf16[512,512]{1,0:T(8,128)(2,1)S(1)}, u32[]{:S(2)}, u32[]{:S(2)}) collective-permute-start(bf16[512,512]{1,0:T(8,128)(2,1)S(1)} %shard_map.79), channel_id=1, source_target_pairs={{8,0},{9,1},{10,2},{11,3},{12,4},{13,5},{14,6},{15,7},{16,8},{17,9... | collective-permute-start | bytes 1572872 | tf_op jit(solution)/shard_map/ppermute | solution.py:217
  37.7 14.3 %collective-permute-start.1 = (bf16[512,512]{1,0:T(8,128)(2,1)S(1)}, bf16[512,512]{1,0:T(8,128)(2,1)S(1)}, u32[]{:S(2)}, u32[]{:S(2)}) collective-permute-start(bf16[512,512]{1,0:T(8,128)(2,1)S(1)} %shard_map.69), channel_id=1, source_target_pairs={{0,1},{1,0},{2,3},{3,2},{4,5},{5,4},{6,7},{7,6},{8,9},{9,8},{10,11... | collective-permute-start | bytes 1572872 | tf_op jit(solution)/shard_map/ppermute | solution.py:217
  39.9 13.6 %collective-permute-start.4 = (bf16[512,512]{1,0:T(8,128)(2,1)S(1)}, bf16[512,512]{1,0:T(8,128)(2,1)S(1)}, u32[]{:S(2)}, u32[]{:S(2)}) collective-permute-start(bf16[512,512]{1,0:T(8,128)(2,1)S(1)} %shard_map.71), channel_id=1, source_target_pairs={{2,4},{3,5},{4,2},{5,3},{10,12},{11,13},{12,10},{13,11},{18,20},{1... | collective-permute-start | bytes 1572872 | tf_op jit(solution)/shard_map/ppermute | solution.py:217
  47.1 16.7 %collective-permute-start.16 = (bf16[512,512]{1,0:T(8,128)(2,1)S(1)}, bf16[512,512]{1,0:T(8,128)(2,1)S(1)}, u32[]{:S(2)}, u32[]{:S(2)}) collective-permute-start(bf16[512,512]{1,0:T(8,128)(2,1)S(1)} %collective-permute-done.15.one.w2), channel_id=1, source_target_pairs={{2,0},{3,1},{4,6},{5,7},{10,8},{11,9},{12,14},{13,15},{18,16},{19,... | collective-permute-start | bytes 1572872 | tf_op jit(solution)/shard_map/ppermute | solution.py:217
  48.4 26.6 %collective-permute-start.18 = (bf16[512,512]{1,0:T(8,128)(2,1)S(1)}, bf16[512,512]{1,0:T(8,128)(2,1)S(1)}, u32[]{:S(2)}, u32[]{:S(2)}) collective-permute-start(bf16[512,512]{1,0:T(8,128)(2,1)S(1)} %collective-permute-done.17.one.w3), channel_id=1, source_target_pairs={{2,0},{3,1},{4,6},{5,7},{10,8},{11,9},{12,14},{13,15},{18,16},{19,... | collective-permute-start | bytes 1572872 | tf_op jit(solution)/shard_map/ppermute | solution.py:217
  50.3 26.9 %collective-permute-start.8 = (bf16[512,512]{1,0:T(8,128)(2,1)S(1)}, bf16[512,512]{1,0:T(8,128)(2,1)S(1)}, u32[]{:S(2)}, u32[]{:S(2)}) collective-permute-start(bf16[512,512]{1,0:T(8,128)(2,1)S(1)} %shard_map.74), channel_id=1, source_target_pairs={{2,4},{3,5},{4,2},{5,3},{10,12},{11,13},{12,10},{13,11},{18,20},{1... | collective-permute-start | bytes 1572872 | tf_op jit(solution)/shard_map/ppermute | solution.py:217
  52.1 34.7 %collective-permute-start.19 = (bf16[256,1024]{1,0:T(8,128)(2,1)S(1)}, bf16[256,1024]{1,0:T(8,128)(2,1)S(1)}, u32[]{:S(2)}, u32[]{:S(2)}) collective-permute-start(bf16[256,1024]{1,0:T(8,128)(2,1)S(1)} %shard_map.80), channel_id=1, source_target_pairs={{0,1},{1,0},{2,3},{3,2},{4,5},{5,4},{6,7},{7,6},{8,9},{9,8},{10,11... | collective-permute-start | bytes 1572872 | tf_op jit(solution)/shard_map/ppermute | solution.py:217
  55.4 25.2 %collective-permute-start.9 = (bf16[256,512]{1,0:T(8,128)(2,1)S(1)}, bf16[256,512]{1,0:T(8,128)(2,1)S(1)}, u32[]{:S(2)}, u32[]{:S(2)}) collective-permute-start(bf16[256,512]{1,0:T(8,128)(2,1)S(1)} %shard_map.76), channel_id=1, source_target_pairs={{0,2},{1,3},{2,0},{3,1},{4,6},{5,7},{6,4},{7,5},{8,10},{9,11},{10,... | collective-permute-start | bytes 786440 | tf_op jit(solution)/shard_map/ppermute | solution.py:217
  63.7 20.2 %collective-permute-start.5 = (bf16[256,512]{1,0:T(8,128)(2,1)S(1)}, bf16[256,512]{1,0:T(8,128)(2,1)S(1)}, u32[]{:S(2)}, u32[]{:S(2)}) collective-permute-start(bf16[256,512]{1,0:T(8,128)(2,1)S(1)} %shard_map.72), channel_id=1, source_target_pairs={{0,2},{1,3},{2,0},{3,1},{4,6},{5,7},{6,4},{7,5},{8,10},{9,11},{10,... | collective-permute-start | bytes 786440 | tf_op jit(solution)/shard_map/ppermute | solution.py:217
  75.0 11.8 %collective-permute-start.20 = (bf16[256,512]{1,0:T(8,128)(2,1)S(1)}, bf16[256,512]{1,0:T(8,128)(2,1)S(1)}, u32[]{:S(2)}, u32[]{:S(2)}) collective-permute-start(bf16[256,512]{1,0:T(8,128)(2,1)S(1)} %shard_map.81), channel_id=1, source_target_pairs={{0,1},{1,0},{2,3},{3,2},{4,5},{5,4},{6,7},{7,6},{8,9},{9,8},{10,11... | collective-permute-start | bytes 786440 | tf_op jit(solution)/shard_map/ppermute | solution.py:217
  77.2 11.1 %collective-permute-start.21 = (bf16[256,512]{1,0:T(8,128)(2,1)S(1)}, bf16[256,512]{1,0:T(8,128)(2,1)S(1)}, u32[]{:S(2)}, u32[]{:S(2)}) collective-permute-start(bf16[256,512]{1,0:T(8,128)(2,1)S(1)} %shard_map.82), channel_id=1, source_target_pairs={{0,1},{1,0},{2,3},{3,2},{4,5},{5,4},{6,7},{7,6},{8,9},{9,8},{10,11... | collective-permute-start | bytes 786440 | tf_op jit(solution)/shard_map/ppermute | solution.py:217
  82.5 10.1 %collective-permute-start.11 = (bf16[256,512]{1,0:T(8,128)(2,1)S(1)}, bf16[256,512]{1,0:T(8,128)(2,1)S(1)}, u32[]{:S(2)}, u32[]{:S(2)}) collective-permute-start(bf16[256,512]{1,0:T(8,128)(2,1)S(1)} %shard_map.77.refs_1_), channel_id=1, source_target_pairs={{0,1},{1,0},{2,3},{3,2},{4,5},{5,4},{6,7},{7,6},{8,9},{9,8},{10,11... | collective-permute-start | bytes 786440 | tf_op jit(solution)/shard_map/ppermute | solution.py:217
  85.8 9.6 %collective-permute-start.10 = (bf16[256,512]{1,0:T(8,128)(2,1)S(1)}, bf16[256,512]{1,0:T(8,128)(2,1)S(1)}, u32[]{:S(2)}, u32[]{:S(2)}) collective-permute-start(bf16[256,512]{1,0:T(8,128)(2,1)S(1)} %shard_map.75.refs_0_), channel_id=1, source_target_pairs={{0,1},{1,0},{2,3},{3,2},{4,5},{5,4},{6,7},{7,6},{8,9},{9,8},{10,11... | collective-permute-start | bytes 786440 | tf_op jit(solution)/shard_map/ppermute | solution.py:217
  (3 other events, 2.4 us)

commit v3 on v2

--- a/solution.py
+++ b/solution.py
@@ -1,7 +1,7 @@
 import functools
+import math
 
 import jax
-import numpy as np
 import jax.numpy as jnp
 from jax import lax
 from jax.experimental import pallas as pl
@@ -103,13 +103,14 @@
     return pl.BlockSpec((flat.shape[0], half), lambda i, ids: (0, ids[slot]))
 
 
-def rotate_body(ids, freq, pos, cot, out):
+def rotate_body(ids, pos, cot, out):
     micro, tokens = pos.shape
     lane = lax.broadcasted_iota(jnp.int32, (tokens, HEAD), 1)
+    freq = jnp.exp(lax.rem(lane, HEAD // 2).astype(F32) * (-2.0 / HEAD * math.log(500000.0)))
     for m in range(micro):
         rows = pl.ds(m * tokens, tokens)
         place = jnp.broadcast_to(pos[pl.ds(m, 1), :].astype(F32), (HEAD, tokens))
-        angle = jnp.transpose(place) * freq[...]
+        angle = jnp.transpose(place) * freq
         cosine = jnp.cos(angle)
         sine = jnp.sin(angle)
         sine = jnp.where(lane < HEAD // 2, sine, -sine)
@@ -137,18 +138,31 @@
     return lax.dot_general(keys, rows, (((1,), (1,)), ((), ())), preferred_element_type=F32)
 
 
-def term_body(slot, at, place, ids, normed, ours, theirs, other, *rest):
-    *sums, out, rows, sem = rest
+def term_body(slot, part, place, ids, normed, ours, theirs, other, *rest):
+    *sums, out, rows, keys, keys_other, rows_other, held, sems = rest
     count, size = rows.shape
-    half = other.shape[1]
-    cols = pl.ds(pl.multiple_of(ids[slot] * half + at, size), size)
-    fetch = pltpu.make_async_copy(normed.at[:, cols], rows, sem)
-    fetch.start()
-    total = outer(other[pl.ds(place * count, count), pl.ds(at, size)], theirs[...])
-    fetch.wait()
-    total = total + outer(rows[...], ours[...])
-    for part in sums:
-        total = total + part[...].astype(F32)
+    at = part * size
+    cols = pl.ds(pl.multiple_of(ids[slot] * other.shape[1] + at, size), size)
+    moves = [
+        (other.at[pl.ds(place * count, count), pl.ds(at, size)], rows_other),
+        (theirs, keys_other),
+        (normed.at[:, cols], rows),
+        (ours, keys),
+    ]
+    for i, add in enumerate(sums):
+        moves.append((add.at[pl.ds(at if add.shape[0] > size else 0, size), :], held.at[i]))
+    copies = [pltpu.make_async_copy(a, b, sems.at[i]) for i, (a, b) in enumerate(moves)]
+    for copy in copies:
+        copy.start()
+    copies[0].wait()
+    copies[1].wait()
+    total = outer(rows_other[...], keys_other[...])
+    copies[2].wait()
+    copies[3].wait()
+    total = total + outer(rows[...], keys[...])
+    for i in range(len(sums)):
+        copies[4 + i].wait()
+        total = total + held[i].astype(F32)
     out[...] = total.astype(out.dtype)
 
 
@@ -187,9 +201,13 @@
     out[...] = (a[...].astype(F32) + b[...].astype(F32)).astype(out.dtype)
 
 
+def last_body(ids, part, held, out):
+    out[...] = part[...]
+
+
 def rows_body(ids, *refs):
     *parts, out = refs
-    count, size = len(parts) // 2, parts[0].shape[0]
+    count, size = PARTS, parts[0].shape[0]
     for i, part in enumerate(parts):
         half = ids[8] if i < count else 1 - ids[8]
         at = pl.multiple_of((half * count + i % count) * size, size)
@@ -223,42 +241,40 @@
     outward = lambda b: {1: 0, 2: 3}.get(b)
 
     last = jnp.where((z == 0) | (z == shards - 1), 3, 2)
-    far = jnp.stack([z, z ^ 1, z ^ (5 - last), z ^ last]).astype(jnp.int32) * replicas
+    line = [b * replicas for b in (z, z ^ 1, z ^ (5 - last), z ^ last)]
+    far = jnp.stack(line).astype(jnp.int32)
     ids = jnp.concatenate([far + y, far + (1 - y), jnp.stack([y, y]).astype(jnp.int32)])
 
     flat = normed.reshape(count, width)
-    index = np.arange(HEAD // 2, dtype=np.float32)
-    freq = np.power(np.float32(500000.0), -2.0 * index / HEAD).astype(np.float32)
-    freq = jnp.asarray(np.concatenate([freq, freq])[None])
-
-    pack0 = lax.dynamic_slice(flat, (0, ids[7] * half), (count, half))
+    pack0 = lax.dynamic_slice(flat, (0, (line[3] + 1 - y) * half), (count, half))
     other0 = send(pack0, stay, swap=1)
-    ours = call(rotate_body, out(count, depth), ids, freq, positions,
+    ours = call(rotate_body, out(count, depth), ids, positions,
                 key_cotangent.reshape(count, depth))
     theirs = send(ours, stay, swap=1)
-    piece = lax.dynamic_slice(key_weight[0], (y * share, 0), (replicas * half - share, depth))
+    piece = call(copy_body, out(half, depth), ids, key_weight[0],
+                 blocks={0: pl.BlockSpec((half, depth), lambda i, ids: (ids[8], 0))})
     w1 = send(piece, flip, back=1)
     w2 = send(piece, across, back=1)
     w0 = send(piece, stay, back=1)
-    pack1 = lax.dynamic_slice(flat, (0, ids[6] * half), (count, half))
+    pack1 = lax.dynamic_slice(flat, (0, (line[2] + 1 - y) * half), (count, half))
     other1 = send(pack1, stay, swap=1)
     pack2 = call(copy_body, out(2 * count, half), ids, flat, flat,
                  blocks={0: block_of(flat, half, 5), 1: block_of(flat, half, 4)})
     other2 = send(pack2, stay, swap=1)
 
-    def term(slot, place, other, *sums, part=0, parts=1, blocks=None):
+    def term(slot, place, other, *sums, part=0, parts=1):
         size = half // parts
-        return call(functools.partial(term_body, slot, part * size, place), out(size, depth), ids,
-                    flat, ours, theirs, other, *sums,
-                    blocks={0: pl.BlockSpec(memory_space=pltpu.HBM)} | (blocks or {}),
-                    scratch=[pltpu.VMEM((count, size), BF16), pltpu.SemaphoreType.DMA],
+        args = (flat, ours, theirs, other, *sums)
+        buffers = [(count, size), (count, depth), (count, depth), (count, size), (max(len(sums), 1), size, depth)]
+        return call(functools.partial(term_body, slot, part, place), out(size, depth), ids, *args,
+                    blocks={i: pl.BlockSpec(memory_space=pltpu.HBM if i == 0 else pl.ANY) for i in range(len(args))},
+                    scratch=[pltpu.VMEM(shape, BF16) for shape in buffers] + [pltpu.SemaphoreType.DMA((len(args),))],
                     flops=4 * count * size * depth)
 
     def plus(a, b):
         return call(add_body, out(*a.shape), ids, a, b)
 
     cut = range(PARTS)
-    part_of = lambda i: pl.BlockSpec((half // PARTS, depth), lambda n, ids: (i, 0))
     term3 = term(3, 0, other0)
     a1 = send(term3, inward)
     w3 = send(w1, across, drop=1)
@@ -270,7 +286,7 @@
     b1 = send(plus(term3, a1), across)
     w5 = send(w3, outward, drop=1)
     b2 = send(plus(term2, a2), across)
-    term1 = [term(1, 0, other2, b1, part=i, parts=PARTS, blocks={4: part_of(i)}) for i in cut]
+    term1 = [term(1, 0, other2, b1, part=i, parts=PARTS) for i in cut]
     c1 = [send(term1[i], flip) for i in cut]
     near = call(share_body, out(count, 2 * share), ids, keys, w0, w1,
                 flops=4 * count * share * depth)
@@ -279,15 +295,15 @@
     mid = send(mid, stay, swap=1)
     far = call(share_pair_body, out(count, share), ids, keys, w3, w5, flops=2 * count * share * depth)
     far = send(far, stay, swap=1)
-    mine = [
-        term(0, 1, other2, c1[i], b2, part=i, parts=PARTS,
-             blocks={5: part_of(i)})
-        for i in cut
-    ]
+    mine = [term(0, 1, other2, c1[i], b2, part=i, parts=PARTS) for i in cut]
     rest = [send(mine[i], stay, swap=1) for i in cut]
     passed = call(passed_body, out(count, width), ids, keys, w0, w1, w2, w4, w3, w5, near, mid, far,
                   flops=2 * count * width * depth)
-    weight_grad = call(rows_body, out(replicas * half, depth), ids, *mine, *rest)
+    rows = call(rows_body, out(replicas * half, depth), ids, *mine, *rest[:-1])
+    size = half // PARTS
+    weight_grad = call(last_body, out(replicas * half, depth), ids, rest[-1], rows,
+                       blocks={1: pl.BlockSpec(memory_space=pl.ANY)}, aliases={2: 0},
+                       place=pl.BlockSpec((size, depth), lambda i, ids: ((1 - ids[8]) * PARTS + PARTS - 1, 0)))
     return weight_grad[None], passed.reshape(normed.shape)
 
 

time: 97.6 us -> 93.5 us (0.958)
  Pallas kernels: 23.2 us -> 19.2 us
  starting transfers between devices: 32.8 us -> 35.5 us
  between operations: 2.25 us -> 0.94 us
    pallas_call x16 -> x18, Pallas kernels: 23.2 us -> 19.2 us  [kernel_call(): pl.pallas_call(body, out_shape=out_shape, grid_spec=pltpu.PrefetchScalarG...]
    ppermute x22, starting transfers between devices: 32.8 us -> 35.5 us  [send(): return lax.ppermute(value, AXES, pairs)]
    unnamed x10 -> x8, local copies, waits for them, and re-layouts: 2.45 us -> 2.97 us
  transfers between devices with their start and end apart: 22 -> 22, of which waited for: 9 -> 10; matrix products, arithmetic and copies ran while one was open for 3% -> 1% of each run, Pallas kernels for 21% -> 18%
where the time goes in v3:
time: 93.5 us; the launch traced here: 93.1 us
  starting transfers between devices  35.5 us (38%)
  waiting for transfers between devices  33.2 us (36%)
  Pallas kernels  19.2 us (21%)
  local copies, waits for them, and re-layouts  4.04 us (4%)
  between operations  0.94 us (1%)
    ppermute x22, starting transfers between devices, send(): return lax.ppermute(value, AXES, pairs)  35.5 us
    ppermute x22, waiting for transfers between devices, send(): return lax.ppermute(value, AXES, pairs)  33.2 us
    pallas_call x18, Pallas kernels, kernel_call(): pl.pallas_call(body, out_shape=out_shape, grid_spec=pltpu.PrefetchScalarG...  19.2 us
    unnamed x8, local copies, waits for them, and re-layouts  2.97 us
  transfers between devices with their start and end apart: 22, of which 10 were waited for; matrix products, arithmetic and copies ran while one was open for 1% of the time, Pallas kernels for 18%

profile of v3, /device:TPU:0, one launch (start us, length us, event | category | flops | bytes accessed | tf_op | source)
XLA Modules:
  0.0 93.1 jit_solution(14866964215738128506)
XLA Ops:
  3.8 3.1 %collective-permute-start = (bf16[256,512]{1,0:T(8,128)(2,1)S(1)}, bf16[256,512]{1,0:T(8,128)(2,1)S(1)}, u32[]{:S(2)}, u32[]{:S(2)}) collective-permute-start(bf16[256,512]{1,0:T(8,128)(2,1)S(1)} %shard_map.59.ours.refs_0_), channel_id=1, source_target_pairs={{0,1},{1,0},{2,3},{3,2},{4,5},{5,4},{6,7},{7,6},{8,9},{9,8},{10,11... | collective-permute-start | bytes 786440 | tf_op jit(solution)/shard_map/ppermute | solution.py:235
  9.8 1.3 %collective-permute-start.14 = (bf16[512,512]{1,0:T(8,128)(2,1)S(1)}, bf16[512,512]{1,0:T(8,128)(2,1)S(1)}, u32[]{:S(2)}, u32[]{:S(2)}) collective-permute-start(bf16[512,512]{1,0:T(8,128)(2,1)S(1)} %shard_map.72), channel_id=1, source_target_pairs={{8,2},{9,3},{10,0},{11,1},{12,6},{13,7},{14,4},{15,5},{16,10},{17,... | collective-permute-start | bytes 1572872 | tf_op jit(solution)/shard_map/ppermute | solution.py:235
  11.8 2.0 %collective-permute-start.6 = (bf16[256,512]{1,0:T(8,128)(2,1)S(1)}, bf16[256,512]{1,0:T(8,128)(2,1)S(1)}, u32[]{:S(2)}, u32[]{:S(2)}) collective-permute-start(bf16[256,512]{1,0:T(8,128)(2,1)S(1)} %get-tuple-element.4), channel_id=1, source_target_pairs={{0,1},{1,0},{2,3},{3,2},{4,5},{5,4},{6,7},{7,6},{8,9},{9,8},{10,11... | collective-permute-start | bytes 786440 | tf_op jit(solution)/shard_map/ppermute | solution.py:235
  14.0 5.6 %collective-permute-done.2.other = bf16[256,512]{1,0:T(8,128)(2,1)S(1)} collective-permute-done((bf16[256,512]{1,0:T(8,128)(2,1)S(1)}, bf16[256,512]{1,0:T(8,128)(2,1)S(1)}, u32[]{:S(2)}, u32[]{:S(2)}) %collective-permute-start.2) | collective-permute-done | bytes 262176 | tf_op jit(solution)/shard_map/ppermute | solution.py:235
  20.8 4.0 %collective-permute-start.3 = (bf16[512,512]{1,0:T(8,128)(2,1)S(1)}, bf16[512,512]{1,0:T(8,128)(2,1)S(1)}, u32[]{:S(2)}, u32[]{:S(2)}) collective-permute-start(bf16[512,512]{1,0:T(8,128)(2,1)S(1)} %shard_map.61.a), channel_id=1, source_target_pairs={{0,2},{1,3},{6,4},{7,5},{8,10},{9,11},{14,12},{15,13},{16,18},{17,... | collective-permute-start | bytes 1572872 | tf_op jit(solution)/shard_map/ppermute | solution.py:235
  24.8 1.3 %collective-permute-start.13 = (bf16[512,512]{1,0:T(8,128)(2,1)S(1)}, bf16[512,512]{1,0:T(8,128)(2,1)S(1)}, u32[]{:S(2)}, u32[]{:S(2)}) collective-permute-start(bf16[512,512]{1,0:T(8,128)(2,1)S(1)} %shard_map.72), channel_id=1, source_target_pairs={{8,0},{9,1},{10,2},{11,3},{12,4},{13,5},{14,6},{15,7},{16,8},{17,9... | collective-permute-start | bytes 1572872 | tf_op jit(solution)/shard_map/ppermute | solution.py:235
  27.3 2.0 %collective-permute-start.7 = (bf16[512,512]{1,0:T(8,128)(2,1)S(1)}, bf16[512,512]{1,0:T(8,128)(2,1)S(1)}, u32[]{:S(2)}, u32[]{:S(2)}) collective-permute-start(bf16[512,512]{1,0:T(8,128)(2,1)S(1)} %shard_map.64.a), channel_id=1, source_target_pairs={{0,2},{1,3},{6,4},{7,5},{8,10},{9,11},{14,12},{15,13},{16,18},{17,... | collective-permute-start | bytes 1572872 | tf_op jit(solution)/shard_map/ppermute | solution.py:235
  30.6 1.3 %collective-permute-start.12 = (bf16[512,512]{1,0:T(8,128)(2,1)S(1)}, bf16[512,512]{1,0:T(8,128)(2,1)S(1)}, u32[]{:S(2)}, u32[]{:S(2)}) collective-permute-start(bf16[512,512]{1,0:T(8,128)(2,1)S(1)} %shard_map.71), channel_id=1, source_target_pairs={{8,0},{9,1},{10,2},{11,3},{12,4},{13,5},{14,6},{15,7},{16,8},{17,9... | collective-permute-start | bytes 1572872 | tf_op jit(solution)/shard_map/ppermute | solution.py:235
  32.5 4.6 %collective-permute-done.3.b = bf16[512,512]{1,0:T(8,128)(2,1)S(1)} collective-permute-done((bf16[512,512]{1,0:T(8,128)(2,1)S(1)}, bf16[512,512]{1,0:T(8,128)(2,1)S(1)}, u32[]{:S(2)}, u32[]{:S(2)}) %collective-permute-start.3) | collective-permute-done | bytes 524320 | tf_op jit(solution)/shard_map/ppermute | solution.py:235
  37.0 1.5 %collective-permute-start.1 = (bf16[512,512]{1,0:T(8,128)(2,1)S(1)}, bf16[512,512]{1,0:T(8,128)(2,1)S(1)}, u32[]{:S(2)}, u32[]{:S(2)}) collective-permute-start(bf16[512,512]{1,0:T(8,128)(2,1)S(1)} %shard_map.60), channel_id=1, source_target_pairs={{0,1},{1,0},{2,3},{3,2},{4,5},{5,4},{6,7},{7,6},{8,9},{9,8},{10,11... | collective-permute-start | bytes 1572872 | tf_op jit(solution)/shard_map/ppermute | solution.py:235
  39.9 5.2 %collective-permute-done.7.b = bf16[512,512]{1,0:T(8,128)(2,1)S(1)} collective-permute-done((bf16[512,512]{1,0:T(8,128)(2,1)S(1)}, bf16[512,512]{1,0:T(8,128)(2,1)S(1)}, u32[]{:S(2)}, u32[]{:S(2)}) %collective-permute-start.7) | collective-permute-done | bytes 524320 | tf_op jit(solution)/shard_map/ppermute | solution.py:235
  45.2 1.3 %collective-permute-start.16 = (bf16[512,512]{1,0:T(8,128)(2,1)S(1)}, bf16[512,512]{1,0:T(8,128)(2,1)S(1)}, u32[]{:S(2)}, u32[]{:S(2)}) collective-permute-start(bf16[512,512]{1,0:T(8,128)(2,1)S(1)} %collective-permute-done.15.one.w2), channel_id=1, source_target_pairs={{2,0},{3,1},{4,6},{5,7},{10,8},{11,9},{12,14},{13,15},{18,16},{19,... | collective-permute-start | bytes 1572872 | tf_op jit(solution)/shard_map/ppermute | solution.py:235
  46.5 1.3 %collective-permute-start.18 = (bf16[512,512]{1,0:T(8,128)(2,1)S(1)}, bf16[512,512]{1,0:T(8,128)(2,1)S(1)}, u32[]{:S(2)}, u32[]{:S(2)}) collective-permute-start(bf16[512,512]{1,0:T(8,128)(2,1)S(1)} %collective-permute-done.17.one.w3), channel_id=1, source_target_pairs={{2,0},{3,1},{4,6},{5,7},{10,8},{11,9},{12,14},{13,15},{18,16},{19,... | collective-permute-start | bytes 1572872 | tf_op jit(solution)/shard_map/ppermute | solution.py:235
  50.2 1.6 %collective-permute-start.19 = (bf16[256,1024]{1,0:T(8,128)(2,1)S(1)}, bf16[256,1024]{1,0:T(8,128)(2,1)S(1)}, u32[]{:S(2)}, u32[]{:S(2)}) collective-permute-start(bf16[256,1024]{1,0:T(8,128)(2,1)S(1)} %shard_map.73), channel_id=1, source_target_pairs={{0,1},{1,0},{2,3},{3,2},{4,5},{5,4},{6,7},{7,6},{8,9},{9,8},{10,11... | collective-permute-start | bytes 1572872 | tf_op jit(solution)/shard_map/ppermute | solution.py:235
  52.8 6.7 %collective-permute-start.10 = (bf16[256,512]{1,0:T(8,128)(2,1)S(1)}, bf16[256,512]{1,0:T(8,128)(2,1)S(1)}, u32[]{:S(2)}, u32[]{:S(2)}) collective-permute-start(bf16[256,512]{1,0:T(8,128)(2,1)S(1)} %shard_map.67), channel_id=1, source_target_pairs={{0,2},{1,3},{2,0},{3,1},{4,6},{5,7},{6,4},{7,5},{8,10},{9,11},{10,... | collective-permute-start | bytes 786440 | tf_op jit(solution)/shard_map/ppermute | solution.py:235
  62.7 10.4 %collective-permute-done.18.two.w5 = bf16[512,512]{1,0:T(8,128)(2,1)S(1)} collective-permute-done((bf16[512,512]{1,0:T(8,128)(2,1)S(1)}, bf16[512,512]{1,0:T(8,128)(2,1)S(1)}, u32[]{:S(2)}, u32[]{:S(2)}) %collective-permute-start.18) | collective-permute-done | bytes 524320 | tf_op jit(solution)/shard_map/ppermute | solution.py:235
  73.1 1.5 %collective-permute-start.20 = (bf16[256,512]{1,0:T(8,128)(2,1)S(1)}, bf16[256,512]{1,0:T(8,128)(2,1)S(1)}, u32[]{:S(2)}, u32[]{:S(2)}) collective-permute-start(bf16[256,512]{1,0:T(8,128)(2,1)S(1)} %shard_map.74), channel_id=1, source_target_pairs={{0,1},{1,0},{2,3},{3,2},{4,5},{5,4},{6,7},{7,6},{8,9},{9,8},{10,11... | collective-permute-start | bytes 786440 | tf_op jit(solution)/shard_map/ppermute | solution.py:235
  76.1 1.6 %collective-permute-done.10.rest_0_ = bf16[256,512]{1,0:T(8,128)(2,1)S(1)} collective-permute-done((bf16[256,512]{1,0:T(8,128)(2,1)S(1)}, bf16[256,512]{1,0:T(8,128)(2,1)S(1)}, u32[]{:S(2)}, u32[]{:S(2)}) %collective-permute-start.10) | collective-permute-done | bytes 262176 | tf_op jit(solution)/shard_map/ppermute | solution.py:235
  78.8 1.6 %collective-permute-start.11 = (bf16[256,512]{1,0:T(8,128)(2,1)S(1)}, bf16[256,512]{1,0:T(8,128)(2,1)S(1)}, u32[]{:S(2)}, u32[]{:S(2)}) collective-permute-start(bf16[256,512]{1,0:T(8,128)(2,1)S(1)} %shard_map.68.refs_0_), channel_id=1, source_target_pairs={{0,1},{1,0},{2,3},{3,2},{4,5},{5,4},{6,7},{7,6},{8,9},{9,8},{10,11... | collective-permute-start | bytes 786440 | tf_op jit(solution)/shard_map/ppermute | solution.py:235
  81.7 1.6 %collective-permute-start.9 = (bf16[256,512]{1,0:T(8,128)(2,1)S(1)}, bf16[256,512]{1,0:T(8,128)(2,1)S(1)}, u32[]{:S(2)}, u32[]{:S(2)}) collective-permute-start(bf16[256,512]{1,0:T(8,128)(2,1)S(1)} %shard_map.66.refs_1_), channel_id=1, source_target_pairs={{0,1},{1,0},{2,3},{3,2},{4,5},{5,4},{6,7},{7,6},{8,9},{9,8},{10,11... | collective-permute-start | bytes 786440 | tf_op jit(solution)/shard_map/ppermute | solution.py:235
  83.3 2.9 %collective-permute-done.21.far = bf16[256,512]{1,0:T(8,128)(2,1)S(1)} collective-permute-done((bf16[256,512]{1,0:T(8,128)(2,1)S(1)}, bf16[256,512]{1,0:T(8,128)(2,1)S(1)}, u32[]{:S(2)}, u32[]{:S(2)}) %collective-permute-start.21) | collective-permute-done | bytes 262176 | tf_op jit(solution)/shard_map/ppermute | solution.py:235
  86.2 2.6 %shard_map.76 = bf16[256,4096]{1,0:T(8,128)(2,1)} custom-call(s32[10]{0:T(128)S(1)} %pad_add_fusion.1.ids, bf16[512,512]{1,0:T(8,128)(2,1)S(1)} %collective-permute-done.12.keys, bf16[512,512]{1,0:T(8,128)(2,1)S(1)} %collective-permute-done.13.rest_0_.w0, bf16[512,512]{1,0:T(8,128)(2,1)S(1)} %collective-permute-done.14.rest_1_.w1, ...), custom_call_target="tpu_custom_call" | custom-call | flops 1073741824 | bytes 4718592 | tf_op jit(solution)/shard_map/pallas_call | solution.py:89
  89.0 1.6 %shard_map.69.held = bf16[1024,512]{1,0:T(8,128)(2,1)} custom-call(s32[10]{0:T(128)S(1)} %pad_add_fusion.1.ids, bf16[256,512]{1,0:T(8,128)(2,1)S(1)} %shard_map.68.refs_0_, bf16[256,512]{1,0:T(8,128)(2,1)S(1)} %shard_map.66.refs_1_, bf16[256,512]{1,0:T(8,128)(2,1)S(1)} %collective-permute-done.11.refs_2_), custom_call_target="tpu_custom_call" | custom-call | bytes 786432 | tf_op jit(solution)/shard_map/pallas_call | solution.py:89
  91.8 1.3 %shard_map.70 = bf16[1024,512]{1,0:T(8,128)(2,1)} custom-call(s32[10]{0:T(128)S(1)} %pad_add_fusion.1.ids, bf16[256,512]{1,0:T(8,128)(2,1)S(1)} %collective-permute-done.9.part, bf16[1024,512]{1,0:T(8,128)(2,1)} %shard_map.69.held), custom_call_target="tpu_custom_call", output_to_operand_aliasing={{}: (2, {})} | custom-call | bytes 262144 | tf_op jit(solution)/shard_map/pallas_call | solution.py:89
  (50 shorter events, 24.3 us)
Async XLA Ops:
  0.6 19.0 %copy-start = (bf16[1,2,128,4096]{3,2,1,0:T(8,128)(2,1)S(1)}, bf16[1,2,128,4096]{3,2,1,0:T(8,128)(2,1)}, u32[]{:S(2)}) copy-start(bf16[1,2,128,4096]{3,2,1,0:T(8,128)(2,1)} %param.4) | copy-start | bytes 6291460
  3.8 10.2 %collective-permute-start = (bf16[256,512]{1,0:T(8,128)(2,1)S(1)}, bf16[256,512]{1,0:T(8,128)(2,1)S(1)}, u32[]{:S(2)}, u32[]{:S(2)}) collective-permute-start(bf16[256,512]{1,0:T(8,128)(2,1)S(1)} %shard_map.59.ours.refs_0_), channel_id=1, source_target_pairs={{0,1},{1,0},{2,3},{3,2},{4,5},{5,4},{6,7},{7,6},{8,9},{9,8},{10,11... | collective-permute-start | bytes 786440 | tf_op jit(solution)/shard_map/ppermute | solution.py:235
  7.9 11.7 %collective-permute-start.2 = (bf16[256,512]{1,0:T(8,128)(2,1)S(1)}, bf16[256,512]{1,0:T(8,128)(2,1)S(1)}, u32[]{:S(2)}, u32[]{:S(2)}) collective-permute-start(bf16[256,512]{1,0:T(8,128)(2,1)S(1)} %get-tuple-element.5), channel_id=1, source_target_pairs={{0,1},{1,0},{2,3},{3,2},{4,5},{5,4},{6,7},{7,6},{8,9},{9,8},{10,11... | collective-permute-start | bytes 786440 | tf_op jit(solution)/shard_map/ppermute | solution.py:235
  8.0 1.2 %copy-start.1 = (bf16[1,1024,512]{2,1,0:T(8,128)(2,1)S(1)}, bf16[1,1024,512]{2,1,0:T(8,128)(2,1)}, u32[]{:S(2)}) copy-start(bf16[1,1024,512]{2,1,0:T(8,128)(2,1)} %param.7) | copy-start | bytes 3145732
  9.8 19.5 %collective-permute-start.14 = (bf16[512,512]{1,0:T(8,128)(2,1)S(1)}, bf16[512,512]{1,0:T(8,128)(2,1)S(1)}, u32[]{:S(2)}, u32[]{:S(2)}) collective-permute-start(bf16[512,512]{1,0:T(8,128)(2,1)S(1)} %shard_map.72), channel_id=1, source_target_pairs={{8,2},{9,3},{10,0},{11,1},{12,6},{13,7},{14,4},{15,5},{16,10},{17,... | collective-permute-start | bytes 1572872 | tf_op jit(solution)/shard_map/ppermute | solution.py:235
  11.1 19.5 %collective-permute-start.15 = (bf16[512,512]{1,0:T(8,128)(2,1)S(1)}, bf16[512,512]{1,0:T(8,128)(2,1)S(1)}, u32[]{:S(2)}, u32[]{:S(2)}) collective-permute-start(bf16[512,512]{1,0:T(8,128)(2,1)S(1)} %shard_map.72), channel_id=1, source_target_pairs={{10,4},{11,5},{12,2},{13,3},{18,12},{19,13},{20,10},{21,11},{26,20... | collective-permute-start | bytes 1572872 | tf_op jit(solution)/shard_map/ppermute | solution.py:235
  11.8 14.3 %collective-permute-start.6 = (bf16[256,512]{1,0:T(8,128)(2,1)S(1)}, bf16[256,512]{1,0:T(8,128)(2,1)S(1)}, u32[]{:S(2)}, u32[]{:S(2)}) collective-permute-start(bf16[256,512]{1,0:T(8,128)(2,1)S(1)} %get-tuple-element.4), channel_id=1, source_target_pairs={{0,1},{1,0},{2,3},{3,2},{4,5},{5,4},{6,7},{7,6},{8,9},{9,8},{10,11... | collective-permute-start | bytes 786440 | tf_op jit(solution)/shard_map/ppermute | solution.py:235
  20.8 16.3 %collective-permute-start.3 = (bf16[512,512]{1,0:T(8,128)(2,1)S(1)}, bf16[512,512]{1,0:T(8,128)(2,1)S(1)}, u32[]{:S(2)}, u32[]{:S(2)}) collective-permute-start(bf16[512,512]{1,0:T(8,128)(2,1)S(1)} %shard_map.61.a), channel_id=1, source_target_pairs={{0,2},{1,3},{6,4},{7,5},{8,10},{9,11},{14,12},{15,13},{16,18},{17,... | collective-permute-start | bytes 1572872 | tf_op jit(solution)/shard_map/ppermute | solution.py:235
  24.8 14.4 %collective-permute-start.13 = (bf16[512,512]{1,0:T(8,128)(2,1)S(1)}, bf16[512,512]{1,0:T(8,128)(2,1)S(1)}, u32[]{:S(2)}, u32[]{:S(2)}) collective-permute-start(bf16[512,512]{1,0:T(8,128)(2,1)S(1)} %shard_map.72), channel_id=1, source_target_pairs={{8,0},{9,1},{10,2},{11,3},{12,4},{13,5},{14,6},{15,7},{16,8},{17,9... | collective-permute-start | bytes 1572872 | tf_op jit(solution)/shard_map/ppermute | solution.py:235
  27.3 17.9 %collective-permute-start.7 = (bf16[512,512]{1,0:T(8,128)(2,1)S(1)}, bf16[512,512]{1,0:T(8,128)(2,1)S(1)}, u32[]{:S(2)}, u32[]{:S(2)}) collective-permute-start(bf16[512,512]{1,0:T(8,128)(2,1)S(1)} %shard_map.64.a), channel_id=1, source_target_pairs={{0,2},{1,3},{6,4},{7,5},{8,10},{9,11},{14,12},{15,13},{16,18},{17,... | collective-permute-start | bytes 1572872 | tf_op jit(solution)/shard_map/ppermute | solution.py:235
  29.3 17.2 %collective-permute-start.17 = (bf16[512,512]{1,0:T(8,128)(2,1)S(1)}, bf16[512,512]{1,0:T(8,128)(2,1)S(1)}, u32[]{:S(2)}, u32[]{:S(2)}) collective-permute-start(bf16[512,512]{1,0:T(8,128)(2,1)S(1)} %collective-permute-done.14.rest_1_.w1), channel_id=1, source_target_pairs={{2,4},{3,5},{4,2},{5,3},{10,12},{11,13},{12,10},{13,11},{18,20},{1... | collective-permute-start | bytes 1572872 | tf_op jit(solution)/shard_map/ppermute | solution.py:235
  30.6 17.9 %collective-permute-start.12 = (bf16[512,512]{1,0:T(8,128)(2,1)S(1)}, bf16[512,512]{1,0:T(8,128)(2,1)S(1)}, u32[]{:S(2)}, u32[]{:S(2)}) collective-permute-start(bf16[512,512]{1,0:T(8,128)(2,1)S(1)} %shard_map.71), channel_id=1, source_target_pairs={{8,0},{9,1},{10,2},{11,3},{12,4},{13,5},{14,6},{15,7},{16,8},{17,9... | collective-permute-start | bytes 1572872 | tf_op jit(solution)/shard_map/ppermute | solution.py:235
  37.0 13.1 %collective-permute-start.1 = (bf16[512,512]{1,0:T(8,128)(2,1)S(1)}, bf16[512,512]{1,0:T(8,128)(2,1)S(1)}, u32[]{:S(2)}, u32[]{:S(2)}) collective-permute-start(bf16[512,512]{1,0:T(8,128)(2,1)S(1)} %shard_map.60), channel_id=1, source_target_pairs={{0,1},{1,0},{2,3},{3,2},{4,5},{5,4},{6,7},{7,6},{8,9},{9,8},{10,11... | collective-permute-start | bytes 1572872 | tf_op jit(solution)/shard_map/ppermute | solution.py:235
  39.2 12.5 %collective-permute-start.4 = (bf16[512,512]{1,0:T(8,128)(2,1)S(1)}, bf16[512,512]{1,0:T(8,128)(2,1)S(1)}, u32[]{:S(2)}, u32[]{:S(2)}) collective-permute-start(bf16[512,512]{1,0:T(8,128)(2,1)S(1)} %shard_map.62), channel_id=1, source_target_pairs={{2,4},{3,5},{4,2},{5,3},{10,12},{11,13},{12,10},{13,11},{18,20},{1... | collective-permute-start | bytes 1572872 | tf_op jit(solution)/shard_map/ppermute | solution.py:235
  45.2 16.7 %collective-permute-start.16 = (bf16[512,512]{1,0:T(8,128)(2,1)S(1)}, bf16[512,512]{1,0:T(8,128)(2,1)S(1)}, u32[]{:S(2)}, u32[]{:S(2)}) collective-permute-start(bf16[512,512]{1,0:T(8,128)(2,1)S(1)} %collective-permute-done.15.one.w2), channel_id=1, source_target_pairs={{2,0},{3,1},{4,6},{5,7},{10,8},{11,9},{12,14},{13,15},{18,16},{19,... | collective-permute-start | bytes 1572872 | tf_op jit(solution)/shard_map/ppermute | solution.py:235
  46.5 26.6 %collective-permute-start.18 = (bf16[512,512]{1,0:T(8,128)(2,1)S(1)}, bf16[512,512]{1,0:T(8,128)(2,1)S(1)}, u32[]{:S(2)}, u32[]{:S(2)}) collective-permute-start(bf16[512,512]{1,0:T(8,128)(2,1)S(1)} %collective-permute-done.17.one.w3), channel_id=1, source_target_pairs={{2,0},{3,1},{4,6},{5,7},{10,8},{11,9},{12,14},{13,15},{18,16},{19,... | collective-permute-start | bytes 1572872 | tf_op jit(solution)/shard_map/ppermute | solution.py:235
  48.5 27.0 %collective-permute-start.8 = (bf16[512,512]{1,0:T(8,128)(2,1)S(1)}, bf16[512,512]{1,0:T(8,128)(2,1)S(1)}, u32[]{:S(2)}, u32[]{:S(2)}) collective-permute-start(bf16[512,512]{1,0:T(8,128)(2,1)S(1)} %shard_map.65), channel_id=1, source_target_pairs={{2,4},{3,5},{4,2},{5,3},{10,12},{11,13},{12,10},{13,11},{18,20},{1... | collective-permute-start | bytes 1572872 | tf_op jit(solution)/shard_map/ppermute | solution.py:235
  50.2 33.1 %collective-permute-start.19 = (bf16[256,1024]{1,0:T(8,128)(2,1)S(1)}, bf16[256,1024]{1,0:T(8,128)(2,1)S(1)}, u32[]{:S(2)}, u32[]{:S(2)}) collective-permute-start(bf16[256,1024]{1,0:T(8,128)(2,1)S(1)} %shard_map.73), channel_id=1, source_target_pairs={{0,1},{1,0},{2,3},{3,2},{4,5},{5,4},{6,7},{7,6},{8,9},{9,8},{10,11... | collective-permute-start | bytes 1572872 | tf_op jit(solution)/shard_map/ppermute | solution.py:235
  52.8 24.8 %collective-permute-start.10 = (bf16[256,512]{1,0:T(8,128)(2,1)S(1)}, bf16[256,512]{1,0:T(8,128)(2,1)S(1)}, u32[]{:S(2)}, u32[]{:S(2)}) collective-permute-start(bf16[256,512]{1,0:T(8,128)(2,1)S(1)} %shard_map.67), channel_id=1, source_target_pairs={{0,2},{1,3},{2,0},{3,1},{4,6},{5,7},{6,4},{7,5},{8,10},{9,11},{10,... | collective-permute-start | bytes 786440 | tf_op jit(solution)/shard_map/ppermute | solution.py:235
  61.9 18.6 %collective-permute-start.5 = (bf16[256,512]{1,0:T(8,128)(2,1)S(1)}, bf16[256,512]{1,0:T(8,128)(2,1)S(1)}, u32[]{:S(2)}, u32[]{:S(2)}) collective-permute-start(bf16[256,512]{1,0:T(8,128)(2,1)S(1)} %shard_map.63), channel_id=1, source_target_pairs={{0,2},{1,3},{2,0},{3,1},{4,6},{5,7},{6,4},{7,5},{8,10},{9,11},{10,... | collective-permute-start | bytes 786440 | tf_op jit(solution)/shard_map/ppermute | solution.py:235
  73.1 10.2 %collective-permute-start.20 = (bf16[256,512]{1,0:T(8,128)(2,1)S(1)}, bf16[256,512]{1,0:T(8,128)(2,1)S(1)}, u32[]{:S(2)}, u32[]{:S(2)}) collective-permute-start(bf16[256,512]{1,0:T(8,128)(2,1)S(1)} %shard_map.74), channel_id=1, source_target_pairs={{0,1},{1,0},{2,3},{3,2},{4,5},{5,4},{6,7},{7,6},{8,9},{9,8},{10,11... | collective-permute-start | bytes 786440 | tf_op jit(solution)/shard_map/ppermute | solution.py:235
  75.5 10.7 %collective-permute-start.21 = (bf16[256,512]{1,0:T(8,128)(2,1)S(1)}, bf16[256,512]{1,0:T(8,128)(2,1)S(1)}, u32[]{:S(2)}, u32[]{:S(2)}) collective-permute-start(bf16[256,512]{1,0:T(8,128)(2,1)S(1)} %shard_map.75), channel_id=1, source_target_pairs={{0,1},{1,0},{2,3},{3,2},{4,5},{5,4},{6,7},{7,6},{8,9},{9,8},{10,11... | collective-permute-start | bytes 786440 | tf_op jit(solution)/shard_map/ppermute | solution.py:235
  78.8 10.2 %collective-permute-start.11 = (bf16[256,512]{1,0:T(8,128)(2,1)S(1)}, bf16[256,512]{1,0:T(8,128)(2,1)S(1)}, u32[]{:S(2)}, u32[]{:S(2)}) collective-permute-start(bf16[256,512]{1,0:T(8,128)(2,1)S(1)} %shard_map.68.refs_0_), channel_id=1, source_target_pairs={{0,1},{1,0},{2,3},{3,2},{4,5},{5,4},{6,7},{7,6},{8,9},{9,8},{10,11... | collective-permute-start | bytes 786440 | tf_op jit(solution)/shard_map/ppermute | solution.py:235
  81.7 10.2 %collective-permute-start.9 = (bf16[256,512]{1,0:T(8,128)(2,1)S(1)}, bf16[256,512]{1,0:T(8,128)(2,1)S(1)}, u32[]{:S(2)}, u32[]{:S(2)}) collective-permute-start(bf16[256,512]{1,0:T(8,128)(2,1)S(1)} %shard_map.66.refs_1_), channel_id=1, source_target_pairs={{0,1},{1,0},{2,3},{3,2},{4,5},{5,4},{6,7},{7,6},{8,9},{9,8},{10,11... | collective-permute-start | bytes 786440 | tf_op jit(solution)/shard_map/ppermute | solution.py:235
  (2 other events, 1.7 us)
